TPU v7x, 768 devices: a whole 4x8x12 slice. The times are simulated.
768 devices in a mesh: group: 4 (over y_lo), blk: 48 (over y_hi, z, core), mp: 4 (over x).
Axes of the slice: x: 4, y: 8 (y_hi: 2, y_lo: 4; y = y_hi * 4 + y_lo), z: 12, core: 2. Of those that a mesh axis runs over, the one named last changes fastest.
Arguments:
- image_hidden: bfloat16 [12288, 1408], P('blk', 'mp'), may hold values from -6 to 6
- image_weight: bfloat16 [1408, 1536], P('mp'), may hold values from -0.00390625 to 0.00390625
- text_embed: bfloat16 [12288, 1536], P(('group', 'blk', 'mp')), may hold values from -0.19921875 to 0.19921875
- positives: int32 [12288], P('blk'), may hold values from 0 to 12287, each once
- log_temp: float32 [1], replicated, may hold values from 1.6 to 3
- bias: float32 [1], replicated, may hold values from -10 to -5
Outputs:
- loss: float32 [1], replicated
- grad_temp: float32 [1], replicated
- grad_bias: float32 [1], replicated
- grad_image: float32 [12288, 1536], P('blk')
- grad_text: float32 [12288, 1536], P(('group', 'blk', 'mp'))
- grad_weight: float32 [1408, 1536], P('mp', ('group', 'blk'))
Inputs may be any that keep to these rules, and one draw needn't show every extreme that they name: positives is a permutation: every text is the positive of exactly one image.
All inputs are finite; a program needn't handle non-finite values.
Results may differ from a plain program's by a relative error of at most 0.0045.
Values may be sent and summed in bfloat16 or wider, within the bound.
No kernel may reach another device: no remote copies, remote signals or barrier semaphores. Data moves between devices by JAX's collectives and lax.ppermute only.
A program may use at most 32 MiB of HBM per device.

v0:
```python
import jax
import jax.numpy as jnp
from jax import lax
from jax.sharding import PartitionSpec as P


def unit_rows(values):
    norm_rows = jnp.sqrt(jnp.sum(values * values, axis=1, keepdims=True) + 1e-06)
    return (values / norm_rows, norm_rows)


def unit_backward(grads, unit, norm_rows):
    return (grads - unit * jnp.sum(unit * grads, axis=1, keepdims=True)) / norm_rows


def on_device(image_hidden, image_weight, text_embed, positives, log_temp, bias):
    groups = lax.axis_size("group")
    blocks = lax.axis_size("blk")
    splits = lax.axis_size("mp")
    share = lax.axis_index("mp")
    group_id = lax.axis_index("group")
    all_rows = image_hidden.shape[0]
    pairs = all_rows * blocks
    partial_value = jnp.dot(image_hidden, image_weight, preferred_element_type=jnp.float32)
    text_unit, text_norm = unit_rows(text_embed.astype(jnp.float32))
    text_low = text_unit.astype(jnp.bfloat16)
    image_emb = lax.psum(partial_value, "mp")
    image_unit, image_norm = unit_rows(image_emb)
    image_low = image_unit.astype(jnp.bfloat16)
    scale = jnp.exp(log_temp[0])
    offset = bias[0]
    width = text_low.shape[0]
    zero = jnp.zeros((), jnp.float32)
    piece = lax.all_gather(text_low, "blk", axis=0, tiled=True)
    loss_sum = zero
    count = piece.shape[0]
    rows_at = lax.iota(jnp.int32, count)
    column = ((group_id * blocks + rows_at // width) * splits + share) * width + rows_at % width
    sims = lax.dot_general(
        image_low, piece, (((1,), (1,)), ((), ())), preferred_element_type=jnp.float32
    )
    logits = scale * sims + offset
    signs = jnp.where(column[None, :] == positives[:, None], 1.0, -1.0).astype(jnp.float32)
    loss_sum = loss_sum - jnp.sum(jax.nn.log_sigmoid(signs * logits))
    slopes = -signs * jax.nn.sigmoid(-signs * logits)
    temp_sum = jnp.sum(slopes * sims)
    bias_sum = jnp.sum(slopes)
    scaled = (scale * slopes).astype(jnp.bfloat16)
    grad_acc = jnp.dot(scaled, piece, preferred_element_type=jnp.float32)
    grad_acc, weights, loss_sum, temp_sum, bias_sum = (
        grad_acc,
        scaled,
        loss_sum,
        temp_sum,
        bias_sum,
    )
    grad_acc = lax.psum(grad_acc, ("group", "mp"))
    loss_sum, temp_sum, bias_sum = lax.psum((loss_sum, temp_sum, bias_sum), ("group", "blk", "mp"))
    grad_image = unit_backward(grad_acc, image_unit, image_norm)
    quarter = all_rows // groups
    first = group_id * quarter
    hidden_rows = lax.dynamic_slice_in_dim(image_hidden, first, quarter, 0)
    grad_low = lax.dynamic_slice_in_dim(grad_image, first, quarter, 0).astype(jnp.bfloat16)
    weight_term = lax.dot_general(
        hidden_rows, grad_low, (((0,), (0,)), ((), ())), preferred_element_type=jnp.float32
    )
    grad_weight = lax.psum_scatter(weight_term, ("group", "blk"), scatter_dimension=1, tiled=True)
    text_sum = lax.psum_scatter(
        lax.dot_general(
            weights, image_low, (((0,), (0,)), ((), ())), preferred_element_type=jnp.float32
        ),
        "blk",
        scatter_dimension=0,
        tiled=True,
    )
    grad_text = unit_backward(text_sum, text_unit, text_norm)
    loss = (loss_sum / pairs).reshape(1)
    grad_temp = (scale * temp_sum / pairs).reshape(1)
    grad_bias = (bias_sum / pairs).reshape(1)
    return (loss, grad_temp, grad_bias, grad_image, grad_text, grad_weight)


def solution(mesh):
    in_specs = (P("blk", "mp"), P("mp", None), P(("group", "blk", "mp"), None), P("blk"), P(), P())
    out_specs = (
        P(),
        P(),
        P(),
        P("blk", None),
        P(("group", "blk", "mp"), None),
        P("mp", ("group", "blk")),
    )
    return jax.shard_map(
        on_device, mesh=mesh, in_specs=in_specs, out_specs=out_specs, check_vma=False
    )
```

profile of v0, /device:TPU:56, one launch (start us, length us, event | category | flops | bytes accessed | tf_op | source)
XLA Modules:
  0.0 680.1 jit_solution(16224622161382805761)
XLA Ops:
  8.0 0.0 copy-start
  8.0 0.0 all-reduce.6.cloned.1.call-start
  8.1 1.2 copy-done
  9.2 2.7 fusion.33
  11.9 0.0 all-reduce.6.cloned.1.call-update
  11.9 0.0 all-gather.2.cloned.1.call-start
  12.0 0.1 fusion.14
  12.1 0.7 fusion.29
  12.8 0.0 all-gather.2.cloned.1.call-update
  12.9 0.0 all-reduce.8.cloned.1.call-start
  14.3 70.6 %all-reduce.6.cloned.1.call-done = f32[256,1536]{1,0:T(8,128)} async-done(((f32[256,1536]{1,0:T(8,128)}), f32[256,1536]{1,0:T(8,128)}) %all-reduce.6.cloned.1.call-update) | async-done | bytes 1572880 | tf_op jit(solution)/shard_map/psum | solution.py:27
  84.9 1.7 multiply_reduce_fusion.1
  86.6 60.6 %all-gather.2.cloned.1.call-done = bf16[768,1536]{1,0:T(8,128)(2,1)} async-done(((bf16[16,1536]{1,0:T(8,128)(2,1)}), bf16[768,1536]{1,0:T(8,128)(2,1)}) %all-gather.2.cloned.1.call-update) | async-done | bytes 2359312 | tf_op jit(solution)/shard_map/all_gather | solution.py:34
  147.2 3.9 fusion.32
  151.1 2.2 fusion.13
  153.2 0.0 all-reduce.8.cloned.1.call-update
  153.2 0.0 all-reduce.10.cloned.1.call-start
  153.3 169.9 %all-reduce.8.cloned.1.call-done = f32[256,1536]{1,0:T(8,128)} async-done(((f32[256,1536]{1,0:T(8,128)}), f32[256,1536]{1,0:T(8,128)}) %all-reduce.8.cloned.1.call-update) | async-done | bytes 1572880 | tf_op jit(solution)/shard_map/psum | solution.py:57
  323.2 1.9 multiply_reduce_fusion
  325.1 0.3 subtract_divide_fusion
  325.5 1.1 copy-done.3
  326.6 2.0 fusion.12
  328.6 0.0 all-reduce.10.cloned.1.call-update
  328.7 0.0 reduce-scatter.2.cloned.1.call-start
  328.7 3.2 fusion.8
  332.0 0.0 reduce-scatter.2.cloned.1.call-update
  332.0 1.3 dynamic-slice
  334.6 122.1 %all-reduce.1 = (f32[]{:T(128)}, f32[]{:T(128)}, f32[]{:T(128)}) all-reduce(f32[]{:T(128)S(6)} %sub.16, f32[]{:T(128)} %get-tuple-element.7, f32[]{:T(128)} %get-tuple-element.6), channel_id=1, replica_groups=mesh['group'=4,'blk'=48,'mp'=4] {'group','blk','mp'}, use_global_device_ids=true, to_apply=%region_4.5 | all-reduce | flops 3 | bytes 24 | tf_op jit(solution)/shard_map/psum | solution.py:58
  458.6 207.0 %all-reduce.10.cloned.1.call-done = f32[352,1536]{0,1:T(8,128)} async-done(((f32[352,1536]{0,1:T(8,128)}), f32[352,1536]{0,1:T(8,128)}) %all-reduce.10.cloned.1.call-update) | async-done | bytes 2162704
  665.6 1.3 constant_dynamic-slice_fusion
  666.9 1.1 multiply_reduce_fusion.3
  668.0 1.6 subtract_divide_fusion.1
  (17 shorter events, 0.1 us)
Async XLA Ops:
  8.0 1.2 copy-start
  8.0 4.0 copy-start.4
  8.0 76.9 %all-reduce.6.cloned.1.call-start = ((), (), s32[]{:S(2)}) async-start(), calls=%async_computation.1 | async-start | bytes 3145728 | tf_op jit(solution)/shard_map/psum | solution.py:27
  11.9 135.3 %copy-start.7 = (s32[256]{0:T(256)S(1)}, s32[256]{0:T(256)}, u32[]{:S(2)}) copy-start(s32[256]{0:T(256)} %param.9) | copy-start | bytes 3076
  11.9 135.3 %all-gather.2.cloned.1.call-start = ((), (), s32[]{:S(2)}) async-start(), calls=%async_computation.2 | async-start | bytes 2408448 | tf_op jit(solution)/shard_map/all_gather | solution.py:34
  12.9 310.4 %all-reduce.8.cloned.1.call-start = ((), (), s32[]{:S(2)}) async-start(), calls=%async_computation.3 | async-start | bytes 3145728 | tf_op jit(solution)/shard_map/psum | solution.py:57
  84.9 62.3 %copy-start.1 = (f32[256,1536]{1,0:T(8,128)S(1)}, f32[256,1536]{1,0:T(8,128)}, u32[]{:S(2)}) copy-start(f32[256,1536]{1,0:T(8,128)} %all-reduce.6.cloned.1.call-done) | copy-start | bytes 4718596
  147.2 3.9 copy-start.6
  153.2 512.3 %all-reduce.10.cloned.1.call-start = ((), (), s32[]{:S(2)}) async-start(), calls=%async_computation.5 | async-start | bytes 4718592
  323.2 1.9 copy-start.2
  325.1 1.5 copy-start.5
  325.5 1.1 copy-start.3
  328.7 338.2 %reduce-scatter.2.cloned.1.call-start = ((), (), s32[]{:S(2)}) async-start(), calls=%async_computation.4 | async-start | bytes 4816896 | tf_op jit(solution)/shard_map/reduce_scatter | solution.py:68
Sparse Core Ops, SparseCore 0:
  12.0 72.8 all-reduce.5
  153.4 169.8 all-reduce.7
  328.8 336.7 all-reduce.9
Sparse Core Ops, SparseCore 1:
  16.7 130.5 all-gather.1
  334.5 203.1 reduce-scatter.1
where the time goes:
time: 683 us; the launch traced here: 680 us
  waiting for transfers between devices  508 us (74%)
  blocking collectives  122 us (18%)
  between operations  23.3 us (3%)
  matrix products  13.9 us (2%)
  other arithmetic  7.5 us (1%)
    unnamed x6, waiting for transfers between devices  207 us
    psum x1, waiting for transfers between devices, on_device(): grad_acc = lax.psum(grad_acc, ('group', 'mp'))  170 us
    psum x1, blocking collectives, on_device(): lax.psum((loss_sum, temp_sum, bias_sum), ('group', 'blk', 'mp'))  122 us
    psum x1, waiting for transfers between devices, on_device(): image_emb = lax.psum(partial_value, 'mp')  70.6 us
    all_gather x1, waiting for transfers between devices, on_device(): piece = lax.all_gather(text_low, 'blk', axis=0, tiled=True)  60.6 us
  transfers between devices with their start and end apart: 5, of which 4 were waited for; matrix products, arithmetic and copies ran while one was open for 1% of the time, Pallas kernels for 0%

commit v1 on v0

v1 whole, which is shorter than its diff:
```python
import jax
import jax.numpy as jnp
from jax import lax
from jax.sharding import Mesh
from jax.sharding import PartitionSpec as P

F32 = jnp.float32
BF16 = jnp.bfloat16


def unit_rows(values):
    norm_rows = jnp.sqrt(jnp.sum(values * values, axis=1, keepdims=True) + 1e-06)
    return (values / norm_rows, norm_rows)


def unit_backward(grads, unit, norm_rows):
    return (grads - unit * jnp.sum(unit * grads, axis=1, keepdims=True)) / norm_rows


def swap(values, axis):
    return lax.ppermute(values, axis, [(0, 1), (1, 0)])


def on_device(image_hidden, image_weight, text_embed, positives, log_temp, bias):
    groups = lax.axis_size("group")
    halves = lax.axis_size("yh")
    rings = lax.axis_size("z")
    cores = lax.axis_size("core")
    splits = lax.axis_size("mp")
    group_id = lax.axis_index("group")
    half = lax.axis_index("yh")
    core = lax.axis_index("core")
    share = lax.axis_index("mp")
    rows = image_hidden.shape[0]
    blocks = halves * rings * cores
    pairs = rows * blocks
    width = text_embed.shape[0]
    embed = text_embed.shape[1]
    hidden = image_hidden.shape[1]

    text_unit, text_norm = unit_rows(text_embed.astype(F32))
    text_low = text_unit.astype(BF16)
    two = lax.all_gather(text_low, "yh", axis=0, tiled=True)
    piece = lax.all_gather(two, "z", axis=0, tiled=True)
    count = piece.shape[0]

    partial_value = jnp.dot(image_hidden, image_weight, preferred_element_type=F32)
    parts = lax.all_to_all(partial_value, "mp", 0, 0, tiled=True)
    quarter = rows // splits
    image_emb = jnp.sum(parts.reshape(splits, quarter, embed), axis=0)
    image_unit, image_norm = unit_rows(image_emb)
    low_own = lax.all_gather(image_unit.astype(BF16), "mp", axis=0, tiled=True)
    low_other = swap(low_own, "core")
    positives_other = swap(positives, "core")

    scale = jnp.exp(log_temp[0])
    offset = bias[0]
    at = lax.iota(jnp.int32, count)
    at_ring, at_half, at_row = at // (halves * width), (at // width) % halves, at % width
    at_block = (at_half * rings + at_ring) * cores + core
    column = ((group_id * blocks + at_block) * splits + share) * width + at_row

    def side(low, wanted):
        sims = lax.dot_general(low, piece, (((1,), (1,)), ((), ())), preferred_element_type=F32)
        logits = scale * sims + offset
        signs = jnp.where(column[None, :] == wanted[:, None], 1.0, -1.0).astype(F32)
        loss_sum = -jnp.sum(jax.nn.log_sigmoid(signs * logits))
        slopes = -signs * jax.nn.sigmoid(-signs * logits)
        temp_sum = jnp.sum(slopes * sims)
        bias_sum = jnp.sum(slopes)
        weights = (scale * slopes).astype(BF16)
        return weights, jnp.stack([loss_sum, temp_sum, bias_sum])

    weights_other, sums_other = side(low_other, positives_other)
    grad_other = jnp.dot(weights_other, piece, preferred_element_type=F32)
    grad_other = swap(grad_other, "core")
    weights_own, sums_own = side(low_own, positives)
    grad_own = jnp.dot(weights_own, piece, preferred_element_type=F32)
    sums = sums_own + sums_other

    text_part = lax.dot_general(
        weights_other, low_other, (((0,), (0,)), ((), ())), preferred_element_type=F32
    ) + lax.dot_general(weights_own, low_own, (((0,), (0,)), ((), ())), preferred_element_type=F32)
    text_two = lax.psum_scatter(text_part, "z", scatter_dimension=0, tiled=True)
    text_two = text_two.reshape(halves, width, embed)
    text_keep = lax.dynamic_index_in_dim(text_two, half, 0, keepdims=False)
    text_send = lax.dynamic_index_in_dim(text_two, 1 - half, 0, keepdims=False)
    text_sum = text_keep + swap(text_send, "yh")
    grad_text = unit_backward(text_sum, text_unit, text_norm)

    grad_acc = grad_own + grad_other
    row_part = jnp.sum(low_own.astype(F32) * grad_acc, axis=1)
    strip = embed // groups
    blocks_out = grad_acc.reshape(splits, quarter, groups, strip).transpose(2, 0, 1, 3)
    extra = jnp.concatenate([row_part.reshape(splits, quarter), jnp.zeros((splits, 128 - quarter), F32), jnp.broadcast_to(jnp.pad(sums, (0, strip - 128 - 3)), (splits, strip - 128))], axis=1)
    extra = jnp.broadcast_to(extra[None, :, None, :], (groups, splits, 8, strip))
    sent = jnp.concatenate([blocks_out, extra], axis=2)
    got = lax.all_to_all(sent.reshape(groups * splits, quarter + 8, strip), ("group", "mp"), 0, 0)
    got = jnp.sum(got.reshape(groups * splits, quarter + 8, strip), axis=0)
    row_sum = got[quarter, :quarter]
    sums = got[quarter, 128:131]
    unit_strip = lax.dynamic_slice_in_dim(image_unit, group_id * strip, strip, 1)
    grad_strip = (got[:quarter] - unit_strip * row_sum[:, None]) / image_norm
    low_strip = lax.all_gather(grad_strip.astype(BF16), "mp", axis=0, tiled=True)
    strips = lax.all_gather(low_strip, "group", axis=0, tiled=False)
    grad_image = strips.transpose(1, 0, 2).reshape(rows, embed).astype(F32)

    weight_part = lax.dot_general(
        low_strip, image_hidden, (((0,), (0,)), ((), ())), preferred_element_type=F32
    )
    lanes = -(-(hidden + 3) // 128) * 128
    tail = jnp.broadcast_to(jnp.pad(sums, (0, lanes - hidden - 3)), (strip, lanes - hidden))
    weight_part = jnp.concatenate([weight_part, tail], axis=1)
    places = halves * rings
    own_cols = strip // blocks
    weight_part = weight_part.reshape(places, cores, own_cols, lanes)
    weight_keep = lax.dynamic_index_in_dim(weight_part, core, 1, keepdims=False)
    weight_send = lax.dynamic_index_in_dim(weight_part, 1 - core, 1, keepdims=False)
    weight_part = weight_keep + swap(weight_send, "core")
    weight_got = lax.all_to_all(weight_part, ("yh", "z"), 0, 0)
    weight_sum = jnp.sum(weight_got.reshape(places, own_cols, lanes), axis=0)
    grad_weight = weight_sum[:, :hidden].T
    loss = (weight_sum[0, hidden] / pairs).reshape(1)
    grad_temp = (scale * weight_sum[0, hidden + 1] / pairs).reshape(1)
    grad_bias = (weight_sum[0, hidden + 2] / pairs).reshape(1)
    return (loss, grad_temp, grad_bias, grad_image, grad_text, grad_weight)


def solution(mesh):
    groups, blocks, splits = (mesh.shape[name] for name in ("group", "blk", "mp"))
    fine = Mesh(
        mesh.devices.reshape(groups, 2, blocks // 4, 2, splits),
        ("group", "yh", "z", "core", "mp"),
    )
    blk = ("yh", "z", "core")
    texts = ("group", *blk, "mp")
    in_specs = (P(blk, "mp"), P("mp", None), P(texts, None), P(blk), P(), P())
    out_specs = (P(), P(), P(), P(blk, None), P(texts, None), P("mp", ("group", *blk)))
    return jax.shard_map(
        on_device, mesh=fine, in_specs=in_specs, out_specs=out_specs, check_vma=False
    )
```

time: 683 us -> 242 us (0.35)
  waiting for transfers between devices: 508 us -> 91.1 us
  blocking collectives: 122 us -> 56.9 us
  starting transfers between devices: 0.21 us -> 37.9 us
    psum x2 -> x0, waiting for transfers between devices: 241 us -> none  [the longest x1 170 us: on_device(): grad_acc = lax.psum(grad_acc, ('group', 'mp'))]
    unnamed x6 -> x2, waiting for transfers between devices: 207 us -> 0.03 us
    psum x1 -> x0, blocking collectives: 122 us -> none  [on_device(): lax.psum((loss_sum, temp_sum, bias_sum), ('group', 'blk', 'mp'))]
    all_gather x0 -> x4, blocking collectives: none -> 56.9 us  [the longest x1 20.1 us: on_device(): strips = lax.all_gather(low_strip, 'group', axis=0, tiled=False)]
    all_to_all x0 -> x3, waiting for transfers between devices: none -> 46.6 us  [the longest x1 35.5 us: on_device(): lax.all_to_all(sent.reshape(groups * splits, quarter + 8, strip), ('group...]
    all_gather x1, waiting for transfers between devices: 60.6 us -> 34 us  [on_device(): piece = lax.all_gather(two, 'z', axis=0, tiled=True)]
    all_to_all x0 -> x3, starting transfers between devices: none -> 24.5 us  [the longest x1 12.4 us: on_device(): weight_got = lax.all_to_all(weight_part, ('yh', 'z'), 0, 0)]
    ppermute x0 -> x5, starting transfers between devices: none -> 13.4 us  [swap(): return lax.ppermute(values, axis, [(0, 1), (1, 0)])]
  transfers between devices with their start and end apart: 5 -> 10, of which waited for: 4 -> 5; matrix products, arithmetic and copies ran while one was open for 1% -> 8% of each run, Pallas kernels for 0% -> 0%
where the time goes in v1:
time: 242 us; the launch traced here: 241 us
  waiting for transfers between devices  91.1 us (38%)
  blocking collectives  56.9 us (24%)
  starting transfers between devices  37.9 us (16%)
  between operations  21 us (9%)
  matrix products  14.8 us (6%)
  other arithmetic  12.1 us (5%)
  local copies, waits for them, and re-layouts  7.31 us (3%)
    all_to_all x1, waiting for transfers between devices, on_device(): lax.all_to_all(sent.reshape(groups * splits, quarter + 8, strip), ('group...  35.5 us
    all_gather x1, waiting for transfers between devices, on_device(): piece = lax.all_gather(two, 'z', axis=0, tiled=True)  34 us
    all_gather x1, blocking collectives, on_device(): strips = lax.all_gather(low_strip, 'group', axis=0, tiled=False)  20.1 us
    all_gather x1, blocking collectives, on_device(): low_own = lax.all_gather(image_unit.astype(BF16), 'mp', axis=0, tiled=True)  14.2 us
    ppermute x5, starting transfers between devices, swap(): return lax.ppermute(values, axis, [(0, 1), (1, 0)])  13.4 us
    all_gather x1, blocking collectives, on_device(): lax.all_gather(grad_strip.astype(BF16), 'mp', axis=0, tiled=True)  13.3 us
    all_to_all x1, starting transfers between devices, on_device(): weight_got = lax.all_to_all(weight_part, ('yh', 'z'), 0, 0)  12.4 us
    all_to_all x1, waiting for transfers between devices, on_device(): parts = lax.all_to_all(partial_value, 'mp', 0, 0, tiled=True)  11.2 us
  transfers between devices with their start and end apart: 10, of which 5 were waited for; matrix products, arithmetic and copies ran while one was open for 8% of the time, Pallas kernels for 0%

profile of v1, /device:TPU:56, one launch (start us, length us, event | category | flops | bytes accessed | tf_op | source)
XLA Modules:
  0.0 241.2 jit_solution(8718271783125094324)
XLA Ops:
  7.2 1.2 copy-done
  8.4 2.7 %fusion.47 = f32[256,1536]{1,0:T(8,128)} fusion(bf16[256,352]{0,1:T(8,128)(2,1)} %param.6, bf16[352,1536]{1,0:T(8,128)(2,1)S(1)} %copy-done), kind=kOutput, calls=%fused_computation.94 | convolution fusion | flops 276824064 | bytes 2834432 | tf_op jit(solution)/shard_map/dot_general | solution.py:47
  11.1 4.4 %all-to-all-start = ((f32[4,64,1536]{2,1,0:T(8,128)}), f32[4,64,1536]{2,1,0:T(8,128)S(1)}, u32[]{:S(2)}, u32[]{:S(2)}) async-start(f32[4,64,1536]{2,1,0:T(8,128)} %bitcast.62), calls=%async_computation | async-start | bytes 3145728 | tf_op jit(solution)/shard_map/all_to_all | solution.py:48
  15.7 9.3 %all_gather.19 = bf16[32,1536]{1,0:T(8,128)(2,1)} all-gather(bf16[16,1536]{1,0:T(8,128)(2,1)S(1)} %fusion.38), channel_id=1, replica_groups=mesh['group'=4,'yh'=2,'z'=12,'core'=2,'mp'=4] {'yh'}, dimensions={0}, use_global_device_ids=true | all-gather | bytes 147456 | tf_op jit(solution)/shard_map/all_gather | solution.py:43
  25.0 11.2 %all-to-all-done = f32[4,64,1536]{2,1,0:T(8,128)S(1)} async-done(((f32[4,64,1536]{2,1,0:T(8,128)}), f32[4,64,1536]{2,1,0:T(8,128)S(1)}, u32[]{:S(2)}, u32[]{:S(2)}) %all-to-all-start) | async-done | bytes 1572896 | tf_op jit(solution)/shard_map/all_to_all | solution.py:48
  37.3 14.2 %all_gather.18 = bf16[256,1536]{1,0:T(8,128)(2,1)S(1)} all-gather(bf16[64,1536]{1,0:T(8,128)(2,1)S(1)} %get-tuple-element.15), channel_id=1, replica_groups=mesh['group'=4,'yh'=2,'z'=12,'core'=2,'mp'=4] {'mp'}, dimensions={0}, use_global_device_ids=true | all-gather | bytes 983040 | tf_op jit(solution)/shard_map/all_gather | solution.py:52
  51.5 1.9 collective-permute-start.1
  53.5 2.4 collective-permute-start
  57.2 34.0 %all-gather.3.cloned.1.call-done = bf16[384,1536]{1,0:T(8,128)(2,1)} async-done(((bf16[32,1536]{1,0:T(8,128)(2,1)}), bf16[384,1536]{1,0:T(8,128)(2,1)}) %all-gather.3.cloned.1.call-update) | async-done | bytes 1179664 | tf_op jit(solution)/shard_map/all_gather | solution.py:44
  91.3 1.9 fusion.48
  93.3 2.0 fusion.15
  96.0 1.9 collective-permute-start.2
  98.0 3.9 %maximum_add_fusion = f32[3]{0:T(128)S(1)} fusion(f32[1]{0:T(128)} %bitcast.6, f32[1]{0:T(128)} %bitcast.5, f32[1]{0:T(128)} %bitcast.4, f32[1]{0:T(128)} %bitcast.9, f32[1]{0:T(128)} %bitcast.8, f32[1]{0:T(128)} %bitcast.7), kind=kLoop, calls=%fused_computation.86 | loop fusion | flops 15 | bytes 36 | tf_op jit(solution)/shard_map/add | solution.py:79
  101.9 2.1 fusion.19
  104.0 1.9 multiply_reduce_fusion
  106.0 1.8 reshape.115
  108.0 1.4 pad_maximum_fusion
  109.4 7.7 %all-to-all-start.1 = ((f32[16,72,384]{2,1,0:T(8,128)}), f32[16,72,384]{2,1,0:T(8,128)}, u32[]{:S(2)}, u32[]{:S(2)}) async-start(f32[16,72,384]{2,1,0:T(8,128)} %bitcast.60), calls=%async_computation.1 | async-start | bytes 3538944 | tf_op jit(solution)/shard_map/all_to_all | solution.py:98
  117.1 3.4 %convolution_add_fusion = f32[384,1536]{1,0:T(8,128)} fusion(f32[384,1536]{1,0:T(8,128)S(1)} %copy-done.1, bf16[256,1536]{1,0:T(8,128)(2,1)} %copy-done.3, f32[]{:T(128)} %bitcast, f32[256,384]{1,0:T(8,128)} %copy-done.7, f32[]{:T(128)} %bitcast.57, s32[384]{0:T(512)S(1)} %fusion.33, s32[256]{0:T(256)S(1)} %collective-permute-done), kind=kOutput, calls=%fused_computation | convolution fusion | flops 303759360 | bytes 5900808 | tf_op jit(solution)/shard_map/dot_general | solution.py:81
  120.5 35.5 %all-to-all-done.1 = f32[16,72,384]{2,1,0:T(8,128)} async-done(((f32[16,72,384]{2,1,0:T(8,128)}), f32[16,72,384]{2,1,0:T(8,128)}, u32[]{:S(2)}, u32[]{:S(2)}) %all-to-all-start.1) | async-done | bytes 1769504 | tf_op jit(solution)/shard_map/all_to_all | solution.py:98
  156.0 1.6 reduce_sum.127
  157.6 1.0 fusion.18
  158.6 13.3 %all_gather.21 = bf16[256,384]{1,0:T(8,128)(2,1)S(1)} all-gather(bf16[64,384]{1,0:T(8,128)(2,1)S(1)} %fusion.18), channel_id=1, replica_groups=mesh['group'=4,'yh'=2,'z'=12,'core'=2,'mp'=4] {'mp'}, dimensions={0}, use_global_device_ids=true | all-gather | bytes 245760 | tf_op jit(solution)/shard_map/all_gather | solution.py:104
  172.6 1.9 collective-permute-start.3
  174.5 4.2 %reduce-scatter.2.cloned.1.call-done = f32[32,1536]{1,0:T(8,128)} async-done(((f32[384,1536]{1,0:T(8,128)}), f32[32,1536]{1,0:T(8,128)}) %reduce-scatter.2.cloned.1.call-update) | async-done | bytes 196624 | tf_op jit(solution)/shard_map/reduce_scatter | solution.py:84
  178.7 1.0 dynamic-slice_bitcast_fusion.1
  179.7 5.2 %collective-permute-start.4 = (f32[16,1536]{1,0:T(8,128)S(1)}, f32[16,1536]{1,0:T(8,128)S(1)}, u32[]{:S(2)}, u32[]{:S(2)}) collective-permute-start(f32[16,1536]{1,0:T(8,128)S(1)} %dynamic-slice_bitcast_fusion.1), channel_id=1, source_target_pairs={{0,96},{96,0},{1,97},{97,1},{2,98},{98,2},{3,99},{99,3},{4,100},{1... | collective-permute-start | bytes 294920 | tf_op jit(solution)/shard_map/ppermute | solution.py:21
  184.9 6.2 %collective-permute-done.4 = f32[16,1536]{1,0:T(8,128)S(1)} collective-permute-done((f32[16,1536]{1,0:T(8,128)S(1)}, f32[16,1536]{1,0:T(8,128)S(1)}, u32[]{:S(2)}, u32[]{:S(2)}) %collective-permute-start.4) | collective-permute-done | bytes 98336 | tf_op jit(solution)/shard_map/ppermute | solution.py:21
  191.1 1.1 multiply_reduce_fusion.4
  193.0 12.4 %all-to-all-start.2 = ((f32[24,8,384]{2,1,0:T(8,128)}), f32[24,8,384]{2,1,0:T(8,128)S(1)}, u32[]{:S(2)}, u32[]{:S(2)}) async-start(f32[24,8,384]{2,1,0:T(8,128)} %bitcast_add_fusion), calls=%async_computation.2 | async-start | bytes 589824 | tf_op jit(solution)/shard_map/all_to_all | solution.py:120
  206.1 20.1 %all-gather = bf16[1024,384]{1,0:T(8,128)(2,1)S(1)} all-gather(bf16[256,384]{1,0:T(8,128)(2,1)S(1)} %all_gather.21), channel_id=2, replica_groups=mesh['group'=4,'yh'=2,'z'=12,'core'=2,'mp'=4] {'group'}, dimensions={0}, use_global_device_ids=true | all-gather | bytes 983040 | tf_op jit(solution)/shard_map/all_gather | solution.py:105
  226.3 1.3 copy.16
  (55 shorter events, 6.2 us)
Async XLA Ops:
  7.2 1.2 copy-start
  11.1 4.4 %copy-start.4 = (bf16[16,1536]{1,0:T(8,128)(2,1)S(1)}, bf16[16,1536]{1,0:T(8,128)(2,1)}, u32[]{:S(2)}) copy-start(bf16[16,1536]{1,0:T(8,128)(2,1)} %param.8) | copy-start | bytes 147460
  11.1 25.1 %all-to-all-start = ((f32[4,64,1536]{2,1,0:T(8,128)}), f32[4,64,1536]{2,1,0:T(8,128)S(1)}, u32[]{:S(2)}, u32[]{:S(2)}) async-start(f32[4,64,1536]{2,1,0:T(8,128)} %bitcast.62), calls=%async_computation | async-start | bytes 3145728 | tf_op jit(solution)/shard_map/all_to_all | solution.py:48
  15.5 75.8 %all-gather.3.cloned.1.call-start = ((), (), s32[]{:S(2)}) async-start(), calls=%async_computation.4 | async-start | bytes 1277952 | tf_op jit(solution)/shard_map/all_gather | solution.py:44
  36.3 17.1 %copy-start.8 = (s32[256]{0:T(256)S(1)}, s32[256]{0:T(256)}, u32[]{:S(2)}) copy-start(s32[256]{0:T(256)} %param.9) | copy-start | bytes 3076
  51.5 41.7 %collective-permute-start.1 = (bf16[256,1536]{1,0:T(8,128)(2,1)S(1)}, bf16[256,1536]{1,0:T(8,128)(2,1)S(1)}, u32[]{:S(2)}, u32[]{:S(2)}) collective-permute-start(bf16[256,1536]{1,0:T(8,128)(2,1)S(1)} %all_gather.18), channel_id=1, source_target_pairs={{0,4},{4,0},{1,5},{5,1},{2,6},{6,2},{3,7},{7,3},{8,12},{12,8},{9,1... | collective-permute-start | bytes 2359304 | tf_op jit(solution)/shard_map/ppermute | solution.py:21
  53.5 39.8 %collective-permute-start = (s32[256]{0:T(256)S(1)}, s32[256]{0:T(256)S(1)}, u32[]{:S(2)}, u32[]{:S(2)}) collective-permute-start(s32[256]{0:T(256)S(1)} %copy-done.8), channel_id=1, source_target_pairs={{0,4},{4,0},{1,5},{5,1},{2,6},{6,2},{3,7},{7,3},{8,12},{12,8},{9,1... | collective-permute-start | bytes 3080 | tf_op jit(solution)/shard_map/ppermute | solution.py:21
  91.3 2.0 copy-start.2
  93.2 2.0 copy-start.3
  95.2 0.8 copy-start.7
  96.0 8.0 %collective-permute-start.2 = (f32[256,1536]{1,0:T(8,128)S(1)}, f32[256,1536]{1,0:T(8,128)S(1)}, u32[]{:S(2)}, u32[]{:S(2)}) collective-permute-start(f32[256,1536]{1,0:T(8,128)S(1)} %fusion.20), channel_id=1, source_target_pairs={{0,4},{4,0},{1,5},{5,1},{2,6},{6,2},{3,7},{7,3},{8,12},{12,8},{9,1... | collective-permute-start | bytes 4718600 | tf_op jit(solution)/shard_map/ppermute | solution.py:21
  109.4 7.7 %copy-start.1 = (f32[384,1536]{1,0:T(8,128)S(1)}, f32[384,1536]{1,0:T(8,128)}, u32[]{:S(2)}) copy-start(f32[384,1536]{1,0:T(8,128)} %fusion.19) | copy-start | bytes 7077892
  109.4 46.6 %all-to-all-start.1 = ((f32[16,72,384]{2,1,0:T(8,128)}), f32[16,72,384]{2,1,0:T(8,128)}, u32[]{:S(2)}, u32[]{:S(2)}) async-start(f32[16,72,384]{2,1,0:T(8,128)} %bitcast.60), calls=%async_computation.1 | async-start | bytes 3538944 | tf_op jit(solution)/shard_map/all_to_all | solution.py:98
  117.0 61.7 %reduce-scatter.2.cloned.1.call-start = ((), (), s32[]{:S(2)}) async-start(), calls=%async_computation.5 | async-start | bytes 2555904 | tf_op jit(solution)/shard_map/reduce_scatter | solution.py:84
  120.5 51.5 %copy-start.5 = (bf16[256,352]{0,1:T(8,128)(2,1)S(1)}, bf16[256,352]{0,1:T(8,128)(2,1)}, u32[]{:S(2)}) copy-start(bf16[256,352]{0,1:T(8,128)(2,1)} %param.6) | copy-start | bytes 540676
  172.6 19.6 %collective-permute-start.3 = (f32[24,8,384]{2,1,0:T(8,128)S(1)}, f32[24,8,384]{2,1,0:T(8,128)S(1)}, u32[]{:S(2)}, u32[]{:S(2)}) collective-permute-start(f32[24,8,384]{2,1,0:T(8,128)S(1)} %dynamic-slice_bitcast_fusion), channel_id=1, source_target_pairs={{0,4},{4,0},{1,5},{5,1},{2,6},{6,2},{3,7},{7,3},{8,12},{12,8},{9,1... | collective-permute-start | bytes 884744 | tf_op jit(solution)/shard_map/ppermute | solution.py:21
  178.7 26.7 %copy-start.6 = (f32[32,1536]{1,0:T(8,128)S(1)}, f32[32,1536]{1,0:T(8,128)}, u32[]{:S(2)}) copy-start(f32[32,1536]{1,0:T(8,128)} %reduce-scatter.2.cloned.1.call-done) | copy-start | bytes 589828
  179.7 11.5 %collective-permute-start.4 = (f32[16,1536]{1,0:T(8,128)S(1)}, f32[16,1536]{1,0:T(8,128)S(1)}, u32[]{:S(2)}, u32[]{:S(2)}) collective-permute-start(f32[16,1536]{1,0:T(8,128)S(1)} %dynamic-slice_bitcast_fusion.1), channel_id=1, source_target_pairs={{0,96},{96,0},{1,97},{97,1},{2,98},{98,2},{3,99},{99,3},{4,100},{1... | collective-permute-start | bytes 294920 | tf_op jit(solution)/shard_map/ppermute | solution.py:21
  193.0 34.7 %all-to-all-start.2 = ((f32[24,8,384]{2,1,0:T(8,128)}), f32[24,8,384]{2,1,0:T(8,128)S(1)}, u32[]{:S(2)}, u32[]{:S(2)}) async-start(f32[24,8,384]{2,1,0:T(8,128)} %bitcast_add_fusion), calls=%async_computation.2 | async-start | bytes 589824 | tf_op jit(solution)/shard_map/all_to_all | solution.py:120
Sparse Core Ops, SparseCore 0:
  25.2 66.0 all-gather.2
  121.0 57.6 reduce-scatter.1

commit v2 on v1

v2 whole, which is shorter than its diff:
```python
import jax
import jax.numpy as jnp
from jax import lax
from jax.sharding import Mesh
from jax.sharding import PartitionSpec as P

F32 = jnp.float32
BF16 = jnp.bfloat16


def unit_rows(values):
    norm_rows = jnp.sqrt(jnp.sum(values * values, axis=1, keepdims=True) + 1e-06)
    return (values / norm_rows, norm_rows)


def unit_backward(grads, unit, norm_rows):
    return (grads - unit * jnp.sum(unit * grads, axis=1, keepdims=True)) / norm_rows


def swap(values, axis):
    return lax.ppermute(values, axis, [(0, 1), (1, 0)])


def shift(values, axes, step):
    size = lax.axis_size(axes)
    return lax.ppermute(values, axes, [(i, (i + step) % size) for i in range(size)])


def exchange(values, axes):
    got = lax.all_to_all(values, axes, 0, 0)
    return got.reshape(values.shape)


def gather(values, axes):
    return exchange(jnp.broadcast_to(values[None], (lax.axis_size(axes), *values.shape)), axes)


RING = ("zs", "zt")
FAR = ("yh", "zs")


def on_device(image_hidden, image_weight, text_embed, positives, log_temp, bias):
    groups = lax.axis_size("group")
    halves = lax.axis_size("yh")
    rings = lax.axis_size(RING)
    turns = lax.axis_size("zt")
    cores = lax.axis_size("core")
    splits = lax.axis_size("mp")
    group_id = lax.axis_index("group")
    turn = lax.axis_index("zt")
    core = lax.axis_index("core")
    share = lax.axis_index("mp")
    rows = image_hidden.shape[0]
    blocks = halves * rings * cores
    pairs = rows * blocks
    width = text_embed.shape[0]
    embed = text_embed.shape[1]
    hidden = image_hidden.shape[1]

    text_unit, text_norm = unit_rows(text_embed.astype(F32))
    text_low = text_unit.astype(BF16)
    with jax.named_scope("text_far"):
        held = gather(text_low, FAR).reshape(-1, embed)
    with jax.named_scope("text_near"):
        after = shift(held, RING, -1)
        before = shift(held, RING, 1)
    piece = jnp.concatenate([held, after, before], axis=0)
    count = piece.shape[0]
    third = held.shape[0]

    image_in, _ = lax.optimization_barrier((image_hidden, text_low))
    quarter = rows // splits

    def partial_for(step):
        place = (share + step) % splits
        chunk = lax.dynamic_slice_in_dim(image_in, place * quarter, quarter, 0)
        return jnp.dot(chunk, image_weight, preferred_element_type=F32)

    with jax.named_scope("image_parts"):
        arrived = [shift(partial_for(step), "mp", step) for step in range(1, splits)]
    image_emb = sum(arrived, partial_for(0))
    image_unit, image_norm = unit_rows(image_emb)
    with jax.named_scope("image_low"):
        lows = gather(image_unit.astype(BF16), ("core", "mp")).reshape(cores, rows, embed)
    low_own = lax.dynamic_index_in_dim(lows, core, 0, keepdims=False)
    low_other = lax.dynamic_index_in_dim(lows, 1 - core, 0, keepdims=False)
    with jax.named_scope("positives"):
        positives_other = swap(positives, "core")

    scale = jnp.exp(log_temp[0])
    offset = bias[0]
    at = lax.iota(jnp.int32, count)
    at_turn = (turn + at // third + jnp.where(at >= 2 * third, turns - 3, 0)) % turns
    at_half, at_step, at_row = at % third // (third // halves), at // width % (rings // turns), at % width
    at_block = (at_half * rings + at_step * turns + at_turn) * cores + core
    column = ((group_id * blocks + at_block) * splits + share) * width + at_row

    def side(low, wanted):
        sims = lax.dot_general(low, piece, (((1,), (1,)), ((), ())), preferred_element_type=F32)
        logits = scale * sims + offset
        signs = jnp.where(column[None, :] == wanted[:, None], 1.0, -1.0).astype(F32)
        losses = -jax.nn.log_sigmoid(signs * logits)
        slopes = -signs * jax.nn.sigmoid(-signs * logits)
        weights = (scale * slopes).astype(BF16)
        return weights, [jnp.sum(v, axis=0) for v in (losses, slopes * sims, slopes)]

    weights_other, sums_other = side(low_other, positives_other)
    grad_other = jnp.dot(weights_other, piece, preferred_element_type=F32)
    low_own, grad_other = lax.optimization_barrier((low_own, grad_other))
    with jax.named_scope("grad_core"):
        grad_other = swap(grad_other, "core")
    weights_own, sums_own = side(low_own, positives)
    grad_own = jnp.dot(weights_own, piece, preferred_element_type=F32)
    weights_other, grad_own = lax.optimization_barrier((weights_other, grad_own))

    text_part = lax.dot_general(
        weights_other, low_other, (((0,), (0,)), ((), ())), preferred_element_type=F32
    ) + lax.dot_general(weights_own, low_own, (((0,), (0,)), ((), ())), preferred_element_type=F32)
    with jax.named_scope("text_back_near"):
        text_held = text_part[:third]
        text_held = text_held + shift(text_part[third : 2 * third], RING, 1)
        text_held = text_held + shift(text_part[2 * third :], RING, -1)

    grad_acc = grad_own + grad_other
    row_part = jnp.sum(low_own.astype(F32) * grad_acc, axis=1)
    strip = embed // groups
    blocks_out = grad_acc.reshape(splits, quarter, groups, strip).transpose(2, 0, 1, 3)
    extra = jnp.zeros((splits, 8, strip), F32)
    extra = extra.at[:, 0, :quarter].set(row_part.reshape(splits, quarter))
    for k in range(3):
        extra = extra.at[:, 1 + k, :count].set((sums_own[k] + sums_other[k])[None])
    extra = jnp.broadcast_to(extra[None], (groups, splits, 8, strip))
    sent = jnp.concatenate([blocks_out, extra], axis=2)
    with jax.named_scope("image_back"):
        got = exchange(sent.reshape(groups * splits, quarter + 8, strip), ("group", "mp"))
    text_held, got = lax.optimization_barrier((text_held, got))
    with jax.named_scope("text_back_far"):
        text_got = exchange(text_held.reshape(-1, width, embed), FAR)
    got = jnp.sum(got, axis=0)
    row_sum = got[quarter, :quarter]
    sums = jnp.sum(got[quarter + 1 : quarter + 4], axis=1)
    unit_strip = lax.dynamic_slice_in_dim(image_unit, group_id * strip, strip, 1)
    grad_strip = (got[:quarter] - unit_strip * row_sum[:, None]) / image_norm
    with jax.named_scope("strip_mp"):
        low_strip = lax.all_gather(grad_strip.astype(BF16), "mp", axis=0, tiled=True)
    with jax.named_scope("strip_group"):
        grad_image = jnp.zeros((rows, embed), F32)
        for step in range(groups):
            strip_from = shift(low_strip, "group", step) if step else low_strip
            place = (group_id - step) % groups * strip
            grad_image = lax.dynamic_update_slice_in_dim(grad_image, strip_from.astype(F32), place, 1)

    weight_part = lax.dot_general(
        low_strip, image_hidden, (((0,), (0,)), ((), ())), preferred_element_type=F32
    )
    lanes = -(-(hidden + 3) // 128) * 128
    tail = jnp.broadcast_to(jnp.pad(sums, (0, lanes - hidden - 3)), (strip, lanes - hidden))
    weight_part = jnp.concatenate([weight_part, tail], axis=1)
    places = halves * rings
    own_cols = strip // blocks
    weight_part = weight_part.reshape(places, cores, own_cols, lanes)
    weight_keep = lax.dynamic_index_in_dim(weight_part, core, 1, keepdims=False)
    weight_send = lax.dynamic_index_in_dim(weight_part, 1 - core, 1, keepdims=False)
    with jax.named_scope("weight_core"):
        weight_part = weight_keep + swap(weight_send, "core")
    weight_part, text_got = lax.optimization_barrier((weight_part, text_got))
    grad_text = unit_backward(jnp.sum(text_got, axis=0), text_unit, text_norm)
    with jax.named_scope("weight_far"):
        weight_sum = jnp.sum(exchange(weight_part, ("yh", *RING)), axis=0)
    grad_weight = weight_sum[:, :hidden].T
    loss = (weight_sum[0, hidden] / pairs).reshape(1)
    grad_temp = (scale * weight_sum[0, hidden + 1] / pairs).reshape(1)
    grad_bias = (weight_sum[0, hidden + 2] / pairs).reshape(1)
    return (loss, grad_temp, grad_bias, grad_image, grad_text, grad_weight)


def solution(mesh):
    groups, blocks, splits = (mesh.shape[name] for name in ("group", "blk", "mp"))
    fine = Mesh(
        mesh.devices.reshape(groups, 2, blocks // 12, 3, 2, splits),
        ("group", "yh", "zs", "zt", "core", "mp"),
    )
    blk = ("yh", "zs", "zt", "core")
    texts = ("group", *blk, "mp")
    in_specs = (P(blk, "mp"), P("mp", None), P(texts, None), P(blk), P(), P())
    out_specs = (P(), P(), P(), P(blk, None), P(texts, None), P("mp", ("group", *blk)))
    return jax.shard_map(
        on_device, mesh=fine, in_specs=in_specs, out_specs=out_specs, check_vma=False
    )
```

time: 242 us -> 240 us (level)
  the two profiles are of different devices: /device:TPU:56 before, /device:TPU:2 now
where the time goes in v2:
time: 240 us; the launch traced here: 239 us
  starting transfers between devices  113 us (47%)
  waiting for transfers between devices  60.8 us (25%)
  other arithmetic  18.3 us (8%)
  blocking collectives  13.9 us (6%)
  matrix products  12.7 us (5%)
  local copies, waits for them, and re-layouts  12.4 us (5%)
  between operations  7.97 us (3%)
    all_to_all x5, starting transfers between devices, exchange(): got = lax.all_to_all(values, axes, 0, 0)  54.2 us
    ppermute x10, starting transfers between devices, shift(): lax.ppermute(values, axes, [(i, (i + step) % size) for i in range(size)])  52.8 us
    all_to_all x5, waiting for transfers between devices, exchange(): got = lax.all_to_all(values, axes, 0, 0)  37 us
    ppermute x10, waiting for transfers between devices, shift(): lax.ppermute(values, axes, [(i, (i + step) % size) for i in range(size)])  23.5 us
    all_gather x1, blocking collectives, on_device(): lax.all_gather(grad_strip.astype(BF16), 'mp', axis=0, tiled=True)  13.9 us
    ppermute x3, starting transfers between devices, swap(): return lax.ppermute(values, axis, [(0, 1), (1, 0)])  5.76 us
    reshape x2, local copies, waits for them, and re-layouts, on_device(): grad_acc.reshape(splits, quarter, groups, strip).transpose(2, 0, 1, 3)  5.47 us
  transfers between devices with their start and end apart: 18, of which 9 were waited for; matrix products, arithmetic and copies ran while one was open for 9% of the time, Pallas kernels for 0%

profile of v2, /device:TPU:2, one launch (start us, length us, event | category | flops | bytes accessed | tf_op | source)
XLA Modules:
  0.0 238.9 jit_solution(6770965599491976755)
XLA Ops:
  3.9 3.4 %collective-permute-start.1 = (f32[64,1536]{1,0:T(8,128)S(1)}, f32[64,1536]{1,0:T(8,128)S(1)}, u32[]{:S(2)}, u32[]{:S(2)}) collective-permute-start(f32[64,1536]{1,0:T(8,128)S(1)} %fusion.32), channel_id=1, source_target_pairs={{0,1},{1,2},{2,3},{3,0},{4,5},{5,6},{6,7},{7,4},{8,9},{9,10},{10,1... | collective-permute-start | bytes 1179656 | tf_op jit(solution)/shard_map/image_parts/ppermute | solution.py:26
  8.5 12.0 %collective-permute-start.2 = (f32[64,1536]{1,0:T(8,128)}, f32[64,1536]{1,0:T(8,128)S(1)}, u32[]{:S(2)}, u32[]{:S(2)}) collective-permute-start(f32[64,1536]{1,0:T(8,128)} %fusion.30), channel_id=1, source_target_pairs={{0,2},{1,3},{2,0},{3,1},{4,6},{5,7},{6,4},{7,5},{8,10},{9,11},{10,... | collective-permute-start | bytes 1179656 | tf_op jit(solution)/shard_map/image_parts/ppermute | solution.py:26
  21.7 1.9 collective-permute-start.3
  24.4 12.9 %all-to-all-start.1 = ((bf16[8,16,1536]{2,1,0:T(8,128)(2,1)}), bf16[8,16,1536]{2,1,0:T(8,128)(2,1)S(1)}, u32[]{:S(2)}, u32[]{:S(2)}) async-start(bf16[8,16,1536]{2,1,0:T(8,128)(2,1)} %broadcast_in_dim.29), calls=%async_computation.1 | async-start | bytes 786432 | tf_op jit(solution)/shard_map/text_far/all_to_all | solution.py:30
  38.8 14.8 %all-to-all-done.1 = bf16[8,16,1536]{2,1,0:T(8,128)(2,1)S(1)} async-done(((bf16[8,16,1536]{2,1,0:T(8,128)(2,1)}), bf16[8,16,1536]{2,1,0:T(8,128)(2,1)S(1)}, u32[]{:S(2)}, u32[]{:S(2)}) %all-to-all-start.1) | async-done | bytes 393248 | tf_op jit(solution)/shard_map/text_far/all_to_all | solution.py:30
  54.9 5.1 %all-to-all-start = ((bf16[8,64,1536]{2,1,0:T(8,128)(2,1)}), bf16[8,64,1536]{2,1,0:T(8,128)(2,1)S(1)}, u32[]{:S(2)}, u32[]{:S(2)}) async-start(bf16[8,64,1536]{2,1,0:T(8,128)(2,1)} %broadcast_in_dim.28), calls=%async_computation | async-start | bytes 3145728 | tf_op jit(solution)/shard_map/image_low/all_to_all | solution.py:30
  59.9 9.7 %collective-permute-start.4 = (bf16[128,1536]{1,0:T(8,128)(2,1)S(1)}, bf16[128,1536]{1,0:T(8,128)(2,1)}, u32[]{:S(2)}, u32[]{:S(2)}) collective-permute-start(bf16[128,1536]{1,0:T(8,128)(2,1)S(1)} %bitcast.51), channel_id=1, source_target_pairs={{0,88},{8,0},{16,8},{24,16},{32,24},{40,32},{48,40},{56,48},{64,56... | collective-permute-start | bytes 1179656 | tf_op jit(solution)/shard_map/text_near/ppermute | solution.py:26
  69.6 3.3 %collective-permute-start.5 = (bf16[128,1536]{1,0:T(8,128)(2,1)S(1)}, bf16[128,1536]{1,0:T(8,128)(2,1)}, u32[]{:S(2)}, u32[]{:S(2)}) collective-permute-start(bf16[128,1536]{1,0:T(8,128)(2,1)S(1)} %bitcast.52), channel_id=1, source_target_pairs={{0,8},{8,16},{16,24},{24,32},{32,40},{40,48},{48,56},{56,64},{64,7... | collective-permute-start | bytes 1179656 | tf_op jit(solution)/shard_map/text_near/ppermute | solution.py:26
  72.9 1.9 collective-permute-start
  76.2 3.3 %all-to-all-done = bf16[8,64,1536]{2,1,0:T(8,128)(2,1)S(1)} async-done(((bf16[8,64,1536]{2,1,0:T(8,128)(2,1)}), bf16[8,64,1536]{2,1,0:T(8,128)(2,1)S(1)}, u32[]{:S(2)}, u32[]{:S(2)}) %all-to-all-start) | async-done | bytes 1572896 | tf_op jit(solution)/shard_map/image_low/all_to_all | solution.py:30
  80.4 3.2 %collective-permute-done.5 = bf16[128,1536]{1,0:T(8,128)(2,1)} collective-permute-done((bf16[128,1536]{1,0:T(8,128)(2,1)S(1)}, bf16[128,1536]{1,0:T(8,128)(2,1)}, u32[]{:S(2)}, u32[]{:S(2)}) %collective-permute-start.5) | collective-permute-done | bytes 393248 | tf_op jit(solution)/shard_map/text_near/ppermute | solution.py:26
  83.7 1.8 multiply_convert_fusion.1
  87.1 1.9 collective-permute-start.8
  90.8 2.0 fusion.35
  95.0 2.8 %reshape.280 = f32[4,64,4,384]{3,2,1,0:T(4,128)} reshape(f32[256,1536]{1,0:T(8,128)} %get-tuple-element.82) | data formatting | bytes 3145728 | tf_op jit(solution)/shard_map/reshape | solution.py:127
  97.8 2.7 %copy.15 = f32[4,64,4,384]{3,1,0,2:T(8,128)} copy(f32[4,64,4,384]{3,2,1,0:T(4,128)} %reshape.280) | data formatting | bytes 3145728 | tf_op jit(solution)/shard_map/reshape | solution.py:127
  100.8 2.8 %pad_maximum_fusion = f32[4,4,72,384]{3,2,1,0:T(8,128)} fusion(f32[4,4,8,384]{3,2,1,0:T(8,128)S(1)} %broadcast_in_dim.31, f32[4,4,64,384]{3,2,1,0:T(8,128)} %bitcast.48), kind=kLoop, calls=%fused_computation.4 | loop fusion | flops 442368 | bytes 3538944 | tf_op jit(solution)/shard_map/concatenate | solution.py:133
  103.6 5.3 %all-to-all-start.2 = ((f32[16,72,384]{2,1,0:T(8,128)}), f32[16,72,384]{2,1,0:T(8,128)}, u32[]{:S(2)}, u32[]{:S(2)}) async-start(f32[16,72,384]{2,1,0:T(8,128)} %bitcast.7), calls=%async_computation.2 | async-start | bytes 3538944 | tf_op jit(solution)/shard_map/image_back/all_to_all | solution.py:30
  112.1 7.5 %collective-permute-start.6 = (f32[128,1536]{1,0:T(8,128)}, f32[128,1536]{1,0:T(8,128)}, u32[]{:S(2)}, u32[]{:S(2)}) collective-permute-start(f32[128,1536]{1,0:T(8,128)} %get-tuple-element.87), channel_id=1, source_target_pairs={{0,8},{8,16},{16,24},{24,32},{32,40},{40,48},{48,56},{56,64},{64,7... | collective-permute-start | bytes 2359304 | tf_op jit(solution)/shard_map/text_back_near/ppermute | solution.py:26
  119.6 1.9 collective-permute-start.7
  121.6 15.3 %collective-permute-done.6 = f32[128,1536]{1,0:T(8,128)} collective-permute-done((f32[128,1536]{1,0:T(8,128)}, f32[128,1536]{1,0:T(8,128)}, u32[]{:S(2)}, u32[]{:S(2)}) %collective-permute-start.6) | collective-permute-done | bytes 786464 | tf_op jit(solution)/shard_map/text_back_near/ppermute | solution.py:26
  136.9 4.1 %collective-permute-done.7 = f32[128,1536]{1,0:T(8,128)} collective-permute-done((f32[128,1536]{1,0:T(8,128)}, f32[128,1536]{1,0:T(8,128)}, u32[]{:S(2)}, u32[]{:S(2)}) %collective-permute-start.7) | collective-permute-done | bytes 786464 | tf_op jit(solution)/shard_map/text_back_near/ppermute | solution.py:26
  141.0 2.4 fusion.2
  146.6 6.5 %all-to-all-start.3 = ((f32[8,16,1536]{2,1,0:T(8,128)}), f32[8,16,1536]{2,1,0:T(8,128)S(1)}, u32[]{:S(2)}, u32[]{:S(2)}) async-start(f32[8,16,1536]{2,1,0:T(8,128)} %bitcast.12), calls=%async_computation.3 | async-start | bytes 1572864 | tf_op jit(solution)/shard_map/text_back_far/all_to_all | solution.py:30
  154.2 13.9 %all_gather.3 = bf16[256,384]{1,0:T(8,128)(2,1)S(1)} all-gather(bf16[64,384]{1,0:T(8,128)(2,1)S(1)} %fusion.27), channel_id=1, replica_groups=mesh['group'=4,'yh'=2,'zs'=4,'zt'=3,'core'=2,'mp'=4] {'mp'}, dimensions={0}, use_global_device_ids=true | all-gather | bytes 245760 | tf_op jit(solution)/shard_map/strip_mp/all_gather | solution.py:145
  168.1 6.7 %collective-permute-start.10 = (bf16[256,384]{1,0:T(8,128)(2,1)S(1)}, bf16[256,384]{1,0:T(8,128)(2,1)}, u32[]{:S(2)}, u32[]{:S(2)}) collective-permute-start(bf16[256,384]{1,0:T(8,128)(2,1)S(1)} %all_gather.3), channel_id=1, source_target_pairs={{0,192},{192,384},{384,576},{576,0},{1,193},{193,385},{385,577},{5... | collective-permute-start | bytes 589832 | tf_op jit(solution)/shard_map/strip_group/ppermute | solution.py:26
  174.8 3.0 %collective-permute-start.11 = (bf16[256,384]{1,0:T(8,128)(2,1)S(1)}, bf16[256,384]{1,0:T(8,128)(2,1)}, u32[]{:S(2)}, u32[]{:S(2)}) collective-permute-start(bf16[256,384]{1,0:T(8,128)(2,1)S(1)} %all_gather.3), channel_id=1, source_target_pairs={{0,384},{192,576},{384,0},{576,192},{1,385},{193,577},{385,1},{577... | collective-permute-start | bytes 589832 | tf_op jit(solution)/shard_map/strip_group/ppermute | solution.py:26
  177.8 3.5 %collective-permute-start.12 = (bf16[256,384]{1,0:T(8,128)(2,1)S(1)}, bf16[256,384]{1,0:T(8,128)(2,1)S(1)}, u32[]{:S(2)}, u32[]{:S(2)}) collective-permute-start(bf16[256,384]{1,0:T(8,128)(2,1)S(1)} %all_gather.3), channel_id=1, source_target_pairs={{0,576},{192,0},{384,192},{576,384},{1,577},{193,1},{385,193},{577... | collective-permute-start | bytes 589832 | tf_op jit(solution)/shard_map/strip_group/ppermute | solution.py:26
  182.1 1.9 collective-permute-start.9
  187.2 24.3 %all-to-all-start.4 = ((f32[24,8,384]{2,1,0:T(8,128)}), f32[24,8,384]{2,1,0:T(8,128)S(1)}, u32[]{:S(2)}, u32[]{:S(2)}) async-start(f32[24,8,384]{2,1,0:T(8,128)} %bitcast_add_fusion), calls=%async_computation.4 | async-start | bytes 589824 | tf_op jit(solution)/shard_map/weight_far/all_to_all | solution.py:30
  211.5 1.7 convert_dynamic-update-slice_fusion.1
  214.9 17.3 %all-to-all-done.4 = f32[24,8,384]{2,1,0:T(8,128)S(1)} async-done(((f32[24,8,384]{2,1,0:T(8,128)}), f32[24,8,384]{2,1,0:T(8,128)S(1)}, u32[]{:S(2)}, u32[]{:S(2)}) %all-to-all-start.4) | async-done | bytes 294944 | tf_op jit(solution)/shard_map/weight_far/all_to_all | solution.py:30
  (84 shorter events, 30.2 us)
Async XLA Ops:
  0.6 2.0 copy-start
  0.6 6.7 %copy-start.3 = (bf16[256,352]{0,1:T(8,128)(2,1)S(1)}, bf16[256,352]{0,1:T(8,128)(2,1)}, u32[]{:S(2)}) copy-start(bf16[256,352]{0,1:T(8,128)(2,1)} %param.14) | copy-start | bytes 540676
  3.9 33.4 %collective-permute-start.1 = (f32[64,1536]{1,0:T(8,128)S(1)}, f32[64,1536]{1,0:T(8,128)S(1)}, u32[]{:S(2)}, u32[]{:S(2)}) collective-permute-start(f32[64,1536]{1,0:T(8,128)S(1)} %fusion.32), channel_id=1, source_target_pairs={{0,1},{1,2},{2,3},{3,0},{4,5},{5,6},{6,7},{7,4},{8,9},{9,10},{10,1... | collective-permute-start | bytes 1179656 | tf_op jit(solution)/shard_map/image_parts/ppermute | solution.py:26
  8.5 28.8 %collective-permute-start.2 = (f32[64,1536]{1,0:T(8,128)}, f32[64,1536]{1,0:T(8,128)S(1)}, u32[]{:S(2)}, u32[]{:S(2)}) collective-permute-start(f32[64,1536]{1,0:T(8,128)} %fusion.30), channel_id=1, source_target_pairs={{0,2},{1,3},{2,0},{3,1},{4,6},{5,7},{6,4},{7,5},{8,10},{9,11},{10,... | collective-permute-start | bytes 1179656 | tf_op jit(solution)/shard_map/image_parts/ppermute | solution.py:26
  21.7 15.6 %collective-permute-start.3 = (f32[64,1536]{1,0:T(8,128)}, f32[64,1536]{1,0:T(8,128)S(1)}, u32[]{:S(2)}, u32[]{:S(2)}) collective-permute-start(f32[64,1536]{1,0:T(8,128)} %fusion.28), channel_id=1, source_target_pairs={{0,3},{1,0},{2,1},{3,2},{4,7},{5,4},{6,5},{7,6},{8,11},{9,8},{10,9... | collective-permute-start | bytes 1179656 | tf_op jit(solution)/shard_map/image_parts/ppermute | solution.py:26
  24.4 29.2 %all-to-all-start.1 = ((bf16[8,16,1536]{2,1,0:T(8,128)(2,1)}), bf16[8,16,1536]{2,1,0:T(8,128)(2,1)S(1)}, u32[]{:S(2)}, u32[]{:S(2)}) async-start(bf16[8,16,1536]{2,1,0:T(8,128)(2,1)} %broadcast_in_dim.29), calls=%async_computation.1 | async-start | bytes 786432 | tf_op jit(solution)/shard_map/text_far/all_to_all | solution.py:30
  54.8 18.0 %copy-start.9 = (s32[256]{0:T(256)S(1)}, s32[256]{0:T(256)}, u32[]{:S(2)}) copy-start(s32[256]{0:T(256)} %param.17) | copy-start | bytes 3076
  54.9 24.7 %all-to-all-start = ((bf16[8,64,1536]{2,1,0:T(8,128)(2,1)}), bf16[8,64,1536]{2,1,0:T(8,128)(2,1)S(1)}, u32[]{:S(2)}, u32[]{:S(2)}) async-start(bf16[8,64,1536]{2,1,0:T(8,128)(2,1)} %broadcast_in_dim.28), calls=%async_computation | async-start | bytes 3145728 | tf_op jit(solution)/shard_map/image_low/all_to_all | solution.py:30
  59.9 20.5 %collective-permute-start.4 = (bf16[128,1536]{1,0:T(8,128)(2,1)S(1)}, bf16[128,1536]{1,0:T(8,128)(2,1)}, u32[]{:S(2)}, u32[]{:S(2)}) collective-permute-start(bf16[128,1536]{1,0:T(8,128)(2,1)S(1)} %bitcast.51), channel_id=1, source_target_pairs={{0,88},{8,0},{16,8},{24,16},{32,24},{40,32},{48,40},{56,48},{64,56... | collective-permute-start | bytes 1179656 | tf_op jit(solution)/shard_map/text_near/ppermute | solution.py:26
  69.6 14.1 %collective-permute-start.5 = (bf16[128,1536]{1,0:T(8,128)(2,1)S(1)}, bf16[128,1536]{1,0:T(8,128)(2,1)}, u32[]{:S(2)}, u32[]{:S(2)}) collective-permute-start(bf16[128,1536]{1,0:T(8,128)(2,1)S(1)} %bitcast.52), channel_id=1, source_target_pairs={{0,8},{8,16},{16,24},{24,32},{32,40},{40,48},{48,56},{56,64},{64,7... | collective-permute-start | bytes 1179656 | tf_op jit(solution)/shard_map/text_near/ppermute | solution.py:26
  72.9 6.7 %collective-permute-start = (s32[256]{0:T(256)S(1)}, s32[256]{0:T(256)S(1)}, u32[]{:S(2)}, u32[]{:S(2)}) collective-permute-start(s32[256]{0:T(256)S(1)} %copy-done.9), channel_id=1, source_target_pairs={{0,4},{4,0},{1,5},{5,1},{2,6},{6,2},{3,7},{7,3},{8,12},{12,8},{9,1... | collective-permute-start | bytes 3080 | tf_op jit(solution)/shard_map/positives/ppermute | solution.py:21
  79.6 14.1 %copy-start.1 = (bf16[256,1536]{1,0:T(8,128)(2,1)}, bf16[256,1536]{1,0:T(8,128)(2,1)S(1)}, u32[]{:S(2)}) copy-start(bf16[256,1536]{1,0:T(8,128)(2,1)S(1)} %dynamic-slice_bitcast_fusion) | copy-start | bytes 2359300
  87.1 6.5 %collective-permute-start.8 = (f32[256,1536]{1,0:T(8,128)S(1)}, f32[256,1536]{1,0:T(8,128)S(1)}, u32[]{:S(2)}, u32[]{:S(2)}) collective-permute-start(f32[256,1536]{1,0:T(8,128)S(1)} %fusion.67), channel_id=1, source_target_pairs={{0,4},{4,0},{1,5},{5,1},{2,6},{6,2},{3,7},{7,3},{8,12},{12,8},{9,1... | collective-permute-start | bytes 4718600 | tf_op jit(solution)/shard_map/grad_core/ppermute | solution.py:21
  90.8 2.0 copy-start.6
  103.6 41.4 %all-to-all-start.2 = ((f32[16,72,384]{2,1,0:T(8,128)}), f32[16,72,384]{2,1,0:T(8,128)}, u32[]{:S(2)}, u32[]{:S(2)}) async-start(f32[16,72,384]{2,1,0:T(8,128)} %bitcast.7), calls=%async_computation.2 | async-start | bytes 3538944 | tf_op jit(solution)/shard_map/image_back/all_to_all | solution.py:30
  108.9 1.1 copy-start.2
  108.9 1.2 copy-start.7
  112.1 24.8 %collective-permute-start.6 = (f32[128,1536]{1,0:T(8,128)}, f32[128,1536]{1,0:T(8,128)}, u32[]{:S(2)}, u32[]{:S(2)}) collective-permute-start(f32[128,1536]{1,0:T(8,128)} %get-tuple-element.87), channel_id=1, source_target_pairs={{0,8},{8,16},{16,24},{24,32},{32,40},{40,48},{48,56},{56,64},{64,7... | collective-permute-start | bytes 2359304 | tf_op jit(solution)/shard_map/text_back_near/ppermute | solution.py:26
  119.6 21.4 %collective-permute-start.7 = (f32[128,1536]{1,0:T(8,128)}, f32[128,1536]{1,0:T(8,128)}, u32[]{:S(2)}, u32[]{:S(2)}) collective-permute-start(f32[128,1536]{1,0:T(8,128)} %get-tuple-element.88), channel_id=1, source_target_pairs={{0,88},{8,0},{16,8},{24,16},{32,24},{40,32},{48,40},{56,48},{64,56... | collective-permute-start | bytes 2359304 | tf_op jit(solution)/shard_map/text_back_near/ppermute | solution.py:26
  143.4 38.1 %copy-start.4 = (bf16[256,352]{0,1:T(8,128)(2,1)S(1)}, bf16[256,352]{0,1:T(8,128)(2,1)}, u32[]{:S(2)}) copy-start(bf16[256,352]{0,1:T(8,128)(2,1)} %param.14) | copy-start | bytes 540676
  146.6 40.5 %all-to-all-start.3 = ((f32[8,16,1536]{2,1,0:T(8,128)}), f32[8,16,1536]{2,1,0:T(8,128)S(1)}, u32[]{:S(2)}, u32[]{:S(2)}) async-start(f32[8,16,1536]{2,1,0:T(8,128)} %bitcast.12), calls=%async_computation.3 | async-start | bytes 1572864 | tf_op jit(solution)/shard_map/text_back_far/all_to_all | solution.py:30
  168.1 16.2 %collective-permute-start.10 = (bf16[256,384]{1,0:T(8,128)(2,1)S(1)}, bf16[256,384]{1,0:T(8,128)(2,1)}, u32[]{:S(2)}, u32[]{:S(2)}) collective-permute-start(bf16[256,384]{1,0:T(8,128)(2,1)S(1)} %all_gather.3), channel_id=1, source_target_pairs={{0,192},{192,384},{384,576},{576,0},{1,193},{193,385},{385,577},{5... | collective-permute-start | bytes 589832 | tf_op jit(solution)/shard_map/strip_group/ppermute | solution.py:26
  174.8 36.7 %collective-permute-start.11 = (bf16[256,384]{1,0:T(8,128)(2,1)S(1)}, bf16[256,384]{1,0:T(8,128)(2,1)}, u32[]{:S(2)}, u32[]{:S(2)}) collective-permute-start(bf16[256,384]{1,0:T(8,128)(2,1)S(1)} %all_gather.3), channel_id=1, source_target_pairs={{0,384},{192,576},{384,0},{576,192},{1,385},{193,577},{385,1},{577... | collective-permute-start | bytes 589832 | tf_op jit(solution)/shard_map/strip_group/ppermute | solution.py:26
  177.8 35.4 %collective-permute-start.12 = (bf16[256,384]{1,0:T(8,128)(2,1)S(1)}, bf16[256,384]{1,0:T(8,128)(2,1)S(1)}, u32[]{:S(2)}, u32[]{:S(2)}) collective-permute-start(bf16[256,384]{1,0:T(8,128)(2,1)S(1)} %all_gather.3), channel_id=1, source_target_pairs={{0,576},{192,0},{384,192},{576,384},{1,577},{193,1},{385,193},{577... | collective-permute-start | bytes 589832 | tf_op jit(solution)/shard_map/strip_group/ppermute | solution.py:26
  182.1 3.5 %collective-permute-start.9 = (f32[24,8,384]{2,1,0:T(8,128)S(1)}, f32[24,8,384]{2,1,0:T(8,128)S(1)}, u32[]{:S(2)}, u32[]{:S(2)}) collective-permute-start(f32[24,8,384]{2,1,0:T(8,128)S(1)} %dynamic-slice_bitcast_fusion.1), channel_id=1, source_target_pairs={{0,4},{4,0},{1,5},{5,1},{2,6},{6,2},{3,7},{7,3},{8,12},{12,8},{9,1... | collective-permute-start | bytes 884744 | tf_op jit(solution)/shard_map/weight_core/ppermute | solution.py:21
  185.3 1.1 copy-start.5
  185.3 28.7 %copy-start.8 = (bf16[16,1536]{1,0:T(8,128)(2,1)S(1)}, bf16[16,1536]{1,0:T(8,128)(2,1)}, u32[]{:S(2)}) copy-start(bf16[16,1536]{1,0:T(8,128)(2,1)} %param.16) | copy-start | bytes 147460
  187.2 45.0 %all-to-all-start.4 = ((f32[24,8,384]{2,1,0:T(8,128)}), f32[24,8,384]{2,1,0:T(8,128)S(1)}, u32[]{:S(2)}, u32[]{:S(2)}) async-start(f32[24,8,384]{2,1,0:T(8,128)} %bitcast_add_fusion), calls=%async_computation.4 | async-start | bytes 589824 | tf_op jit(solution)/shard_map/weight_far/all_to_all | solution.py:30

commit v3 on v2

v3 whole, which is shorter than its diff:
```python
import functools

import jax
import jax.numpy as jnp
from jax import lax
from jax.experimental import pallas as pl
from jax.experimental.pallas import tpu as pltpu
from jax.sharding import Mesh
from jax.sharding import PartitionSpec as P


F32 = jnp.float32
BF16 = jnp.bfloat16


def unit_rows(values):
    norm_rows = jnp.sqrt(jnp.sum(values * values, axis=1, keepdims=True) + 1e-06)
    return (values / norm_rows, norm_rows)


def unit_backward(grads, unit, norm_rows):
    return (grads - unit * jnp.sum(unit * grads, axis=1, keepdims=True)) / norm_rows


def swap(values, axis):
    return lax.ppermute(values, axis, [(0, 1), (1, 0)])


def shift(values, axes, step):
    size = lax.axis_size(axes)
    return lax.ppermute(values, axes, [(i, (i + step) % size) for i in range(size)])


def exchange(values, axes):
    got = lax.all_to_all(values, axes, 0, 0)
    return got.reshape(values.shape)


def gather(values, axes):
    return exchange(jnp.broadcast_to(values[None], (lax.axis_size(axes), *values.shape)), axes)


NT = (((1,), (1,)), ((), ()))


def side_kernel(sizes, factors, ids, low, held, after, before, wanted, earlier, weights, sent, totals):
    groups, splits, quarter, strip, halves, rings, turns, cores, width = sizes
    scale, offset = factors[0], factors[1]
    group_id, turn, core, share = ids[0], ids[1], ids[2], ids[3]
    blocks = halves * rings * cores
    third = held.shape[0]
    rows = low.shape[0]
    low_rows = low[...]
    wanted_row = wanted[...]
    grads = jnp.zeros((rows, low.shape[1]), F32)
    row_part = jnp.zeros((1, rows), F32)
    sums = [jnp.zeros((1, rows), F32)] * 3
    for k, piece in enumerate((held, after, before)):
        texts = piece[...]
        at = lax.broadcasted_iota(jnp.int32, (third, rows), 0)
        at_turn = lax.rem(turn + (0, 1, turns - 1)[k], turns)
        steps = rings // turns
        at_place = at // width
        at_block = ((at_place // steps) * rings + (at_place % steps) * turns + at_turn) * cores + core
        column = ((group_id * blocks + at_block) * splits + share) * width + at % width
        sims = lax.dot_general(texts, low_rows, NT, preferred_element_type=F32)
        logits = scale * sims + offset
        signs = jnp.where(column == wanted_row, 1.0, -1.0).astype(F32)
        x = -signs * logits
        small = jnp.exp(-jnp.abs(x))
        losses = jnp.maximum(x, 0.0) + jnp.log1p(small)
        slopes = -signs * (jnp.where(x >= 0, 1.0, small) / (1.0 + small))
        value = (scale * slopes).astype(BF16)
        weights[k * third : (k + 1) * third, :] = value
        value = value.astype(F32)
        grads = grads + lax.dot_general(
            value.T.astype(BF16), texts, (((1,), (0,)), ((), ())), preferred_element_type=F32
        )
        row_part = row_part + jnp.sum(value * sims, axis=0, keepdims=True)
        for i, v in enumerate((losses, slopes * sims, slopes)):
            sums[i] = sums[i] + jnp.sum(v, axis=0, keepdims=True)
    sums = jnp.concatenate(sums, axis=0) + earlier[0:3, :]
    totals[...] = jnp.concatenate([sums, jnp.zeros((5, rows), F32)], axis=0)
    low_wide = low_rows.astype(F32)
    grads = grads - low_wide * jnp.sum(low_wide * grads, axis=1, keepdims=True)
    lines = [row_part]
    if sent.dtype == F32:
        for k in range(3):
            high = sums[k : k + 1].astype(BF16).astype(F32)
            lines += [high, sums[k : k + 1] - high]
    more = jnp.concatenate([*lines, jnp.zeros((16 - len(lines), rows), F32)], axis=0)
    if strip > rows:
        more = jnp.concatenate([more, jnp.zeros((16, strip - rows), F32)], axis=1)
    for g in range(groups):
        for m in range(splits):
            block = grads[m * quarter : (m + 1) * quarter, g * strip : (g + 1) * strip]
            sent[g * splits + m, :quarter, :] = block.astype(sent.dtype)
            sent[g * splits + m, quarter:, :] = more.astype(sent.dtype)


def text_kernel(weights_own, low_own, weights_other, low_other, held, after, before, *outs):
    third, embed = held.shape
    for k, (piece, out) in enumerate(zip((held, after, before), outs)):
        at = slice(k * third, (k + 1) * third)
        grads = jnp.dot(
            weights_own[at, :], low_own[...], preferred_element_type=F32
        ) + jnp.dot(weights_other[at, :], low_other[...], preferred_element_type=F32)
        texts = piece[...].astype(F32)
        row_part = jnp.sum(texts * grads, axis=1, keepdims=True)
        out[:, :embed] = (grads - texts * row_part).astype(out.dtype)
        out[:, embed:] = jnp.broadcast_to(row_part, (third, 128)).astype(out.dtype)


RING = ("zs", "zt")
FAR = ("yh", "zs")


def on_device(image_hidden, image_weight, text_embed, positives, log_temp, bias):
    groups = lax.axis_size("group")
    halves = lax.axis_size("yh")
    rings = lax.axis_size(RING)
    turns = lax.axis_size("zt")
    cores = lax.axis_size("core")
    splits = lax.axis_size("mp")
    group_id = lax.axis_index("group")
    turn = lax.axis_index("zt")
    core = lax.axis_index("core")
    share = lax.axis_index("mp")
    rows = image_hidden.shape[0]
    blocks = halves * rings * cores
    pairs = rows * blocks
    width = text_embed.shape[0]
    embed = text_embed.shape[1]
    hidden = image_hidden.shape[1]

    text_unit, text_norm = unit_rows(text_embed.astype(F32))
    text_low = text_unit.astype(BF16)
    held = gather(text_low, FAR).reshape(-1, embed)
    after = shift(held, RING, -1)
    before = shift(held, RING, 1)
    third = held.shape[0]

    quarter = rows // splits

    def partial_for(step):
        place = (share + step) % splits
        chunk = lax.dynamic_slice_in_dim(image_hidden, place * quarter, quarter, 0)
        return jnp.dot(chunk, image_weight, preferred_element_type=F32)

    arrived = [shift(partial_for(step), "mp", step) for step in range(1, splits)]
    image_emb = sum(arrived, partial_for(0))
    image_unit, image_norm = unit_rows(image_emb)
    image_low = image_unit.astype(BF16)
    low_own = lax.all_gather(image_low, "mp", axis=0, tiled=True)
    low_other = swap(low_own, "core")
    positives_other = swap(positives, "core")

    scale = jnp.exp(log_temp[0])
    strip = embed // groups
    factors = jnp.concatenate([jnp.exp(log_temp), bias])
    ids = jnp.stack([group_id, turn, core, share]).astype(jnp.int32)
    sizes = (groups, splits, quarter, strip, halves, rings, turns, cores, width)
    smem = pl.BlockSpec(memory_space=pltpu.SMEM)
    vmem = pl.BlockSpec(memory_space=pltpu.VMEM)

    def side(low, wanted, earlier, kind):
        return pl.pallas_call(
            functools.partial(side_kernel, sizes),
            out_shape=(
                jax.ShapeDtypeStruct((3 * third, rows), BF16),
                jax.ShapeDtypeStruct((groups * splits, quarter + 16, strip), kind),
                jax.ShapeDtypeStruct((8, rows), F32),
            ),
            in_specs=[smem, smem, vmem, vmem, vmem, vmem, vmem, vmem],
            out_specs=(vmem, vmem, vmem),
            name="side",
        )(factors, ids, low, held, after, before, wanted.reshape(1, rows), earlier)

    weights_other, sent_other, totals = side(
        low_other, positives_other, jnp.zeros((8, rows), F32), BF16
    )
    sent_other = swap(sent_other, "core")
    weights_own, sent_own, _ = side(low_own, positives, totals, F32)
    sent = (sent_own + sent_other.astype(F32)).astype(BF16)
    weights_other, sent = lax.optimization_barrier((weights_other, sent))

    text_held, text_after, text_before = pl.pallas_call(
        text_kernel,
        out_shape=tuple(jax.ShapeDtypeStruct((third, embed + 128), k) for k in (F32, BF16, BF16)),
        in_specs=[vmem] * 7,
        out_specs=(vmem,) * 3,
        name="text_part",
    )(weights_own, low_own, weights_other, low_other, held, after, before)
    text_after = shift(text_after, RING, 1).astype(F32)
    text_before = shift(text_before, RING, -1).astype(F32)
    text_held = (text_held + text_after + text_before).astype(BF16)

    got = exchange(sent, ("group", "mp"))
    text_held, got = lax.optimization_barrier((text_held, got))
    text_got = exchange(text_held.reshape(-1, width, embed + 128), FAR)
    got = jnp.sum(got.astype(F32), axis=0)
    row_sum = lax.dynamic_slice_in_dim(got[quarter], share * quarter, quarter, 0)
    sums = jnp.sum(got[quarter + 1 : quarter + 7].reshape(3, 2 * strip), axis=1)
    unit_strip = lax.dynamic_slice_in_dim(image_unit, group_id * strip, strip, 1)
    off = unit_strip.astype(BF16).astype(F32) - unit_strip
    grad_strip = (got[:quarter] + off * row_sum[:, None]) / image_norm
    low_strip = lax.all_gather(grad_strip.astype(BF16), "mp", axis=0, tiled=True)
    grad_image = jnp.zeros((rows, embed), F32)
    for step in range(groups):
        strip_from = shift(low_strip, "group", step) if step else low_strip
        place = (group_id - step) % groups * strip
        grad_image = lax.dynamic_update_slice_in_dim(grad_image, strip_from.astype(F32), place, 1)

    weight_part = lax.dot_general(
        low_strip, image_hidden, (((0,), (0,)), ((), ())), preferred_element_type=F32
    )
    lanes = -(-(hidden + 3) // 128) * 128
    tail = jnp.broadcast_to(jnp.pad(sums, (0, lanes - hidden - 3)), (strip, lanes - hidden))
    weight_part = jnp.concatenate([weight_part, tail], axis=1)
    places = halves * rings
    own_cols = strip // blocks
    weight_part = weight_part.reshape(places, cores, own_cols, lanes)
    weight_keep = lax.dynamic_index_in_dim(weight_part, core, 1, keepdims=False)
    weight_send = lax.dynamic_index_in_dim(weight_part, 1 - core, 1, keepdims=False)
    weight_part = weight_keep + swap(weight_send, "core")
    weight_part, text_got = lax.optimization_barrier((weight_part, text_got))
    text_got = jnp.sum(text_got.astype(F32), axis=0)
    text_sum = text_got[:, :embed] + text_low.astype(F32) * text_got[:, embed : embed + 1]
    grad_text = unit_backward(text_sum, text_unit, text_norm)
    weight_sum = jnp.sum(exchange(weight_part, ("yh", *RING)), axis=0)
    grad_weight = weight_sum[:, :hidden].T
    loss = (weight_sum[0, hidden] / pairs).reshape(1)
    grad_temp = (scale * weight_sum[0, hidden + 1] / pairs).reshape(1)
    grad_bias = (weight_sum[0, hidden + 2] / pairs).reshape(1)
    return (loss, grad_temp, grad_bias, grad_image, grad_text, grad_weight)


def solution(mesh):
    groups, blocks, splits = (mesh.shape[name] for name in ("group", "blk", "mp"))
    fine = Mesh(
        mesh.devices.reshape(groups, 2, blocks // 12, 3, 2, splits),
        ("group", "yh", "zs", "zt", "core", "mp"),
    )
    blk = ("yh", "zs", "zt", "core")
    texts = ("group", *blk, "mp")
    in_specs = (P(blk, "mp"), P("mp", None), P(texts, None), P(blk), P(), P())
    out_specs = (P(), P(), P(), P(blk, None), P(texts, None), P("mp", ("group", *blk)))
    return jax.shard_map(
        on_device, mesh=fine, in_specs=in_specs, out_specs=out_specs, check_vma=False
    )
```

time: 240 us -> 208 us (0.87)
  starting transfers between devices: 113 us -> 90.8 us
  waiting for transfers between devices: 60.8 us -> 45.3 us
  Pallas kernels: 0 us -> 14.1 us
  blocking collectives: 13.9 us -> 25.4 us
  matrix products: 12.7 us -> 4.42 us
  local copies, waits for them, and re-layouts: 12.4 us -> 5.84 us
  other arithmetic: 18.3 us -> 13.1 us
    all_to_all x5 -> x4, starting transfers between devices: 54.2 us -> 37 us  [exchange(): got = lax.all_to_all(values, axes, 0, 0)]
    pallas_call x0 -> x3, Pallas kernels: none -> 14.1 us  [the longest x2 10.3 us: side(): pl.pallas_call(functools.partial(side_kernel, sizes), out_shape=(jax.Shap...]
    all_gather x0 -> x1, blocking collectives: none -> 13.3 us  [on_device(): low_own = lax.all_gather(image_low, 'mp', axis=0, tiled=True)]
    dot_general x6 -> x0, matrix products: 8.3 us -> none  [the longest x2 3.48 us: side(): lax.dot_general(low, piece, (((1,), (1,)), ((), ())), preferred_element_t...]
    ppermute x10, waiting for transfers between devices: 23.5 us -> 15.7 us  [shift(): lax.ppermute(values, axes, [(i, (i + step) % size) for i in range(size)])]
    all_to_all x5 -> x4, waiting for transfers between devices: 37 us -> 29.5 us  [exchange(): got = lax.all_to_all(values, axes, 0, 0)]
    ppermute x10, starting transfers between devices: 52.8 us -> 46.2 us  [shift(): lax.ppermute(values, axes, [(i, (i + step) % size) for i in range(size)])]
    reshape x2 -> x0, local copies, waits for them, and re-layouts: 5.47 us -> none  [on_device(): grad_acc.reshape(splits, quarter, groups, strip).transpose(2, 0, 1, 3)]
  transfers between devices with their start and end apart: 18 -> 18, of which waited for: 9 -> 6; matrix products, arithmetic and copies ran while one was open for 9% -> 6% of each run, Pallas kernels for 0% -> 4%
where the time goes in v3:
time: 208 us; the launch traced here: 207 us
  starting transfers between devices  90.8 us (44%)
  waiting for transfers between devices  45.3 us (22%)
  blocking collectives  25.4 us (12%)
  Pallas kernels  14.1 us (7%)
  other arithmetic  13.1 us (6%)
  between operations  7.79 us (4%)
  local copies, waits for them, and re-layouts  5.84 us (3%)
  matrix products  4.42 us (2%)
    ppermute x10, starting transfers between devices, shift(): lax.ppermute(values, axes, [(i, (i + step) % size) for i in range(size)])  46.2 us
    all_to_all x4, starting transfers between devices, exchange(): got = lax.all_to_all(values, axes, 0, 0)  37 us
    all_to_all x4, waiting for transfers between devices, exchange(): got = lax.all_to_all(values, axes, 0, 0)  29.5 us
    ppermute x10, waiting for transfers between devices, shift(): lax.ppermute(values, axes, [(i, (i + step) % size) for i in range(size)])  15.7 us
    all_gather x1, blocking collectives, on_device(): low_own = lax.all_gather(image_low, 'mp', axis=0, tiled=True)  13.3 us
    all_gather x1, blocking collectives, on_device(): lax.all_gather(grad_strip.astype(BF16), 'mp', axis=0, tiled=True)  12.2 us
    pallas_call x2, Pallas kernels, side(): pl.pallas_call(functools.partial(side_kernel, sizes), out_shape=(jax.Shap...  10.3 us
    ppermute x4, starting transfers between devices, swap(): return lax.ppermute(values, axis, [(0, 1), (1, 0)])  7.66 us
  transfers between devices with their start and end apart: 18, of which 6 were waited for; matrix products, arithmetic and copies ran while one was open for 6% of the time, Pallas kernels for 4%

profile of v3, /device:TPU:2, one launch (start us, length us, event | category | flops | bytes accessed | tf_op | source)
XLA Modules:
  0.0 206.8 jit_solution(1795434636225117302)
XLA Ops:
  0.7 1.2 copy-done
  1.9 1.3 fusion.5
  3.2 11.4 %collective-permute-start.2 = (f32[64,1536]{1,0:T(8,128)S(1)}, f32[64,1536]{1,0:T(8,128)S(1)}, u32[]{:S(2)}, u32[]{:S(2)}) collective-permute-start(f32[64,1536]{1,0:T(8,128)S(1)} %fusion.5), channel_id=1, source_target_pairs={{0,3},{1,0},{2,1},{3,2},{4,7},{5,4},{6,5},{7,6},{8,11},{9,8},{10,9... | collective-permute-start | bytes 1179656 | tf_op jit(solution)/shard_map/ppermute | solution.py:31
  15.8 1.9 collective-permute-start.1
  18.9 3.4 %collective-permute-start = (f32[64,1536]{1,0:T(8,128)}, f32[64,1536]{1,0:T(8,128)S(1)}, u32[]{:S(2)}, u32[]{:S(2)}) collective-permute-start(f32[64,1536]{1,0:T(8,128)} %fusion.9), channel_id=1, source_target_pairs={{0,1},{1,2},{2,3},{3,0},{4,5},{5,6},{6,7},{7,4},{8,9},{9,10},{10,1... | collective-permute-start | bytes 1179656 | tf_op jit(solution)/shard_map/ppermute | solution.py:31
  23.3 13.5 %all-to-all-start = ((bf16[8,16,1536]{2,1,0:T(8,128)(2,1)}), bf16[8,16,1536]{2,1,0:T(8,128)(2,1)S(1)}, u32[]{:S(2)}, u32[]{:S(2)}) async-start(bf16[8,16,1536]{2,1,0:T(8,128)(2,1)} %broadcast_in_dim.8), calls=%async_computation | async-start | bytes 786432 | tf_op jit(solution)/shard_map/all_to_all | solution.py:35
  38.3 13.3 %all_gather.6.low.low_own = bf16[256,1536]{1,0:T(8,128)(2,1)S(1)} all-gather(bf16[64,1536]{1,0:T(8,128)(2,1)S(1)} %get-tuple-element.34), channel_id=1, replica_groups=mesh['group'=4,'yh'=2,'zs'=4,'zt'=3,'core'=2,'mp'=4] {'mp'}, dimensions={0}, use_global_device_ids=true | all-gather | bytes 983040 | tf_op jit(solution)/shard_map/all_gather | solution.py:154
  51.5 1.9 collective-permute-start.5
  53.5 9.3 %collective-permute-start.3 = (bf16[128,1536]{1,0:T(8,128)(2,1)S(1)}, bf16[128,1536]{1,0:T(8,128)(2,1)S(1)}, u32[]{:S(2)}, u32[]{:S(2)}) collective-permute-start(bf16[128,1536]{1,0:T(8,128)(2,1)S(1)} %bitcast.28), channel_id=1, source_target_pairs={{0,88},{8,0},{16,8},{24,16},{32,24},{40,32},{48,40},{56,48},{64,56... | collective-permute-start | bytes 1179656 | tf_op jit(solution)/shard_map/ppermute | solution.py:31
  62.8 3.2 %collective-permute-start.4 = (bf16[128,1536]{1,0:T(8,128)(2,1)S(1)}, bf16[128,1536]{1,0:T(8,128)(2,1)S(1)}, u32[]{:S(2)}, u32[]{:S(2)}) collective-permute-start(bf16[128,1536]{1,0:T(8,128)(2,1)S(1)} %bitcast.29), channel_id=1, source_target_pairs={{0,8},{8,16},{16,24},{24,32},{32,40},{40,48},{48,56},{56,64},{64,7... | collective-permute-start | bytes 1179656 | tf_op jit(solution)/shard_map/ppermute | solution.py:31
  66.1 1.9 collective-permute-start.6
  71.1 4.2 %collective-permute-done.4.before = bf16[128,1536]{1,0:T(8,128)(2,1)S(1)} collective-permute-done((bf16[128,1536]{1,0:T(8,128)(2,1)S(1)}, bf16[128,1536]{1,0:T(8,128)(2,1)S(1)}, u32[]{:S(2)}, u32[]{:S(2)}) %collective-permute-start.4) | collective-permute-done | bytes 393248 | tf_op jit(solution)/shard_map/ppermute | solution.py:31
  76.0 5.0 %side.2 = (bf16[384,256]{1,0:T(8,128)(2,1)}, bf16[16,80,384]{2,1,0:T(8,128)(2,1)}, f32[8,256]{1,0:T(8,128)}) custom-call(f32[2]{0:T(128)} %pad_maximum_fusion.1.factors, s32[4]{0:T(128)} %pad_add_fusion.ids, bf16[256,1536]{1,0:T(8,128)(2,1)} %collective-permute-done.5.low.low_other, bf16[128,1536]{1,0:T(8,128)(2,1)} %bitcast.30, ...), custom_call_target="tpu_custom_call" | custom-call | tf_op jit(solution)/shard_map/side/pallas_call | solution.py:167
  81.0 1.9 collective-permute-start.7
  82.9 5.3 %side.3 = (bf16[384,256]{1,0:T(8,128)(2,1)}, f32[16,80,384]{2,1,0:T(8,128)}, f32[8,256]{1,0:T(8,128)}) custom-call(f32[2]{0:T(128)} %pad_maximum_fusion.1.factors, s32[4]{0:T(128)} %pad_add_fusion.ids, bf16[256,1536]{1,0:T(8,128)(2,1)} %copy-done.1, bf16[128,1536]{1,0:T(8,128)(2,1)} %bitcast.31, bf16[128,1536]{1,0:T(8,128)(2,1)} %copy-done.3, ...), custom_call_target="tpu_custom_call" | custom-call | tf_op jit(solution)/shard_map/side/pallas_call | solution.py:167
  88.2 2.7 %add_convert_fusion = bf16[16,80,384]{2,1,0:T(8,128)(2,1)} fusion(f32[16,80,384]{2,1,0:T(8,128)} %get-tuple-element.23, bf16[16,80,384]{2,1,0:T(8,128)(2,1)S(1)} %collective-permute-done.7), kind=kLoop, calls=%fused_computation.4 | loop fusion | flops 1474560 | bytes 3932160 | tf_op jit(solution)/shard_map/convert_element_type | solution.py:184
  90.9 9.4 %all-to-all-start.1 = ((bf16[16,80,384]{2,1,0:T(8,128)(2,1)}), bf16[16,80,384]{2,1,0:T(8,128)(2,1)S(1)}, u32[]{:S(2)}, u32[]{:S(2)}) async-start(bf16[16,80,384]{2,1,0:T(8,128)(2,1)} %add_convert_fusion), calls=%async_computation.1 | async-start | bytes 1966080 | tf_op jit(solution)/shard_map/all_to_all | solution.py:35
  100.3 3.9 %text_part.1 = (f32[128,1664]{1,0:T(8,128)}, bf16[128,1664]{1,0:T(8,128)(2,1)}, bf16[128,1664]{1,0:T(8,128)(2,1)}) custom-call(bf16[384,256]{1,0:T(8,128)(2,1)} %get-tuple-element.21.weights_own, bf16[256,1536]{1,0:T(8,128)(2,1)} %copy-done.1, bf16[384,256]{1,0:T(8,128)(2,1)} %get-tuple-element.25.weights_other, ...), custom_call_target="tpu_custom_call" | custom-call | tf_op jit(solution)/shard_map/text_part/pallas_call | solution.py:187
  104.1 1.9 collective-permute-start.9
  106.1 3.9 %collective-permute-start.8 = (bf16[128,1664]{1,0:T(8,128)(2,1)}, bf16[128,1664]{1,0:T(8,128)(2,1)S(1)}, u32[]{:S(2)}, u32[]{:S(2)}) collective-permute-start(bf16[128,1664]{1,0:T(8,128)(2,1)} %get-tuple-element.27), channel_id=1, source_target_pairs={{0,8},{8,16},{16,24},{24,32},{32,40},{40,48},{48,56},{56,64},{64,7... | collective-permute-start | bytes 1277960 | tf_op jit(solution)/shard_map/ppermute | solution.py:31
  110.1 7.8 %collective-permute-done.9 = bf16[128,1664]{1,0:T(8,128)(2,1)S(1)} collective-permute-done((bf16[128,1664]{1,0:T(8,128)(2,1)}, bf16[128,1664]{1,0:T(8,128)(2,1)S(1)}, u32[]{:S(2)}, u32[]{:S(2)}) %collective-permute-start.9) | collective-permute-done | bytes 426016 | tf_op jit(solution)/shard_map/ppermute | solution.py:31
  117.9 3.1 %collective-permute-done.8 = bf16[128,1664]{1,0:T(8,128)(2,1)S(1)} collective-permute-done((bf16[128,1664]{1,0:T(8,128)(2,1)}, bf16[128,1664]{1,0:T(8,128)(2,1)S(1)}, u32[]{:S(2)}, u32[]{:S(2)}) %collective-permute-start.8) | collective-permute-done | bytes 426016 | tf_op jit(solution)/shard_map/ppermute | solution.py:31
  121.0 2.0 add_convert_fusion.1
  124.4 12.2 %all_gather.7 = bf16[256,384]{1,0:T(8,128)(2,1)S(1)} all-gather(bf16[64,384]{1,0:T(8,128)(2,1)S(1)} %fusion.4), channel_id=1, replica_groups=mesh['group'=4,'yh'=2,'zs'=4,'zt'=3,'core'=2,'mp'=4] {'mp'}, dimensions={0}, use_global_device_ids=true | all-gather | bytes 245760 | tf_op jit(solution)/shard_map/all_gather | solution.py:207
  136.8 4.4 %collective-permute-start.11 = (bf16[256,384]{1,0:T(8,128)(2,1)S(1)}, bf16[256,384]{1,0:T(8,128)(2,1)}, u32[]{:S(2)}, u32[]{:S(2)}) collective-permute-start(bf16[256,384]{1,0:T(8,128)(2,1)S(1)} %all_gather.7), channel_id=1, source_target_pairs={{0,192},{192,384},{384,576},{576,0},{1,193},{193,385},{385,577},{5... | collective-permute-start | bytes 589832 | tf_op jit(solution)/shard_map/ppermute | solution.py:31
  141.2 3.3 %collective-permute-start.12 = (bf16[256,384]{1,0:T(8,128)(2,1)S(1)}, bf16[256,384]{1,0:T(8,128)(2,1)}, u32[]{:S(2)}, u32[]{:S(2)}) collective-permute-start(bf16[256,384]{1,0:T(8,128)(2,1)S(1)} %all_gather.7), channel_id=1, source_target_pairs={{0,384},{192,576},{384,0},{576,192},{1,385},{193,577},{385,1},{577... | collective-permute-start | bytes 589832 | tf_op jit(solution)/shard_map/ppermute | solution.py:31
  144.5 3.4 %collective-permute-start.13 = (bf16[256,384]{1,0:T(8,128)(2,1)S(1)}, bf16[256,384]{1,0:T(8,128)(2,1)S(1)}, u32[]{:S(2)}, u32[]{:S(2)}) collective-permute-start(bf16[256,384]{1,0:T(8,128)(2,1)S(1)} %all_gather.7), channel_id=1, source_target_pairs={{0,576},{192,0},{384,192},{576,384},{1,577},{193,1},{385,193},{577... | collective-permute-start | bytes 589832 | tf_op jit(solution)/shard_map/ppermute | solution.py:31
  148.2 5.3 %all-to-all-start.2 = ((bf16[8,16,1664]{2,1,0:T(8,128)(2,1)}), bf16[8,16,1664]{2,1,0:T(8,128)(2,1)S(1)}, u32[]{:S(2)}, u32[]{:S(2)}) async-start(bf16[8,16,1664]{2,1,0:T(8,128)(2,1)} %bitcast.11), calls=%async_computation.2 | async-start | bytes 851968 | tf_op jit(solution)/shard_map/all_to_all | solution.py:35
  153.9 1.9 collective-permute-start.10
  159.9 12.2 %all-to-all-done.2 = bf16[8,16,1664]{2,1,0:T(8,128)(2,1)S(1)} async-done(((bf16[8,16,1664]{2,1,0:T(8,128)(2,1)}), bf16[8,16,1664]{2,1,0:T(8,128)(2,1)S(1)}, u32[]{:S(2)}, u32[]{:S(2)}) %all-to-all-start.2) | async-done | bytes 426016 | tf_op jit(solution)/shard_map/all_to_all | solution.py:35
  172.1 8.9 %all-to-all-start.3 = ((f32[24,8,384]{2,1,0:T(8,128)}), f32[24,8,384]{2,1,0:T(8,128)S(1)}, u32[]{:S(2)}, u32[]{:S(2)}) async-start(f32[24,8,384]{2,1,0:T(8,128)} %bitcast_add_fusion), calls=%async_computation.3 | async-start | bytes 589824 | tf_op jit(solution)/shard_map/all_to_all | solution.py:35
  182.9 17.4 %all-to-all-done.3 = f32[24,8,384]{2,1,0:T(8,128)S(1)} async-done(((f32[24,8,384]{2,1,0:T(8,128)}), f32[24,8,384]{2,1,0:T(8,128)S(1)}, u32[]{:S(2)}, u32[]{:S(2)}) %all-to-all-start.3) | async-done | bytes 294944 | tf_op jit(solution)/shard_map/all_to_all | solution.py:35
  (69 shorter events, 16.7 us)
Async XLA Ops:
  0.6 1.2 copy-start
  0.6 14.0 %copy-start.5 = (bf16[256,352]{0,1:T(8,128)(2,1)S(1)}, bf16[256,352]{0,1:T(8,128)(2,1)}, u32[]{:S(2)}) copy-start(bf16[256,352]{0,1:T(8,128)(2,1)} %param.6) | copy-start | bytes 540676
  3.2 33.6 %collective-permute-start.2 = (f32[64,1536]{1,0:T(8,128)S(1)}, f32[64,1536]{1,0:T(8,128)S(1)}, u32[]{:S(2)}, u32[]{:S(2)}) collective-permute-start(f32[64,1536]{1,0:T(8,128)S(1)} %fusion.5), channel_id=1, source_target_pairs={{0,3},{1,0},{2,1},{3,2},{4,7},{5,4},{6,5},{7,6},{8,11},{9,8},{10,9... | collective-permute-start | bytes 1179656 | tf_op jit(solution)/shard_map/ppermute | solution.py:31
  14.6 7.7 %copy-start.7 = (bf16[16,1536]{1,0:T(8,128)(2,1)S(1)}, bf16[16,1536]{1,0:T(8,128)(2,1)}, u32[]{:S(2)}) copy-start(bf16[16,1536]{1,0:T(8,128)(2,1)} %param.8) | copy-start | bytes 147460
  15.8 21.0 %collective-permute-start.1 = (f32[64,1536]{1,0:T(8,128)}, f32[64,1536]{1,0:T(8,128)S(1)}, u32[]{:S(2)}, u32[]{:S(2)}) collective-permute-start(f32[64,1536]{1,0:T(8,128)} %fusion.7), channel_id=1, source_target_pairs={{0,2},{1,3},{2,0},{3,1},{4,6},{5,7},{6,4},{7,5},{8,10},{9,11},{10,... | collective-permute-start | bytes 1179656 | tf_op jit(solution)/shard_map/ppermute | solution.py:31
  18.9 17.9 %collective-permute-start = (f32[64,1536]{1,0:T(8,128)}, f32[64,1536]{1,0:T(8,128)S(1)}, u32[]{:S(2)}, u32[]{:S(2)}) collective-permute-start(f32[64,1536]{1,0:T(8,128)} %fusion.9), channel_id=1, source_target_pairs={{0,1},{1,2},{2,3},{3,0},{4,5},{5,6},{6,7},{7,4},{8,9},{9,10},{10,1... | collective-permute-start | bytes 1179656 | tf_op jit(solution)/shard_map/ppermute | solution.py:31
  23.3 30.2 %all-to-all-start = ((bf16[8,16,1536]{2,1,0:T(8,128)(2,1)}), bf16[8,16,1536]{2,1,0:T(8,128)(2,1)S(1)}, u32[]{:S(2)}, u32[]{:S(2)}) async-start(bf16[8,16,1536]{2,1,0:T(8,128)(2,1)} %broadcast_in_dim.8), calls=%async_computation | async-start | bytes 786432 | tf_op jit(solution)/shard_map/all_to_all | solution.py:35
  37.4 28.7 %copy-start.8 = (s32[256]{0:T(256)S(1)}, s32[256]{0:T(256)}, u32[]{:S(2)}) copy-start(s32[256]{0:T(256)} %param.9) | copy-start | bytes 3076
  51.5 31.4 %copy-start.1 = (bf16[256,1536]{1,0:T(8,128)(2,1)}, bf16[256,1536]{1,0:T(8,128)(2,1)S(1)}, u32[]{:S(2)}) copy-start(bf16[256,1536]{1,0:T(8,128)(2,1)S(1)} %all_gather.6.low.low_own) | copy-start | bytes 2359300
  51.5 19.0 %collective-permute-start.5 = (bf16[256,1536]{1,0:T(8,128)(2,1)S(1)}, bf16[256,1536]{1,0:T(8,128)(2,1)}, u32[]{:S(2)}, u32[]{:S(2)}) collective-permute-start(bf16[256,1536]{1,0:T(8,128)(2,1)S(1)} %all_gather.6.low.low_own), channel_id=1, source_target_pairs={{0,4},{4,0},{1,5},{5,1},{2,6},{6,2},{3,7},{7,3},{8,12},{12,8},{9,1... | collective-permute-start | bytes 2359304 | tf_op jit(solution)/shard_map/ppermute | solution.py:26
  53.5 22.4 %copy-start.2 = (bf16[8,16,1536]{2,1,0:T(8,128)(2,1)}, bf16[8,16,1536]{2,1,0:T(8,128)(2,1)S(1)}, u32[]{:S(2)}) copy-start(bf16[8,16,1536]{2,1,0:T(8,128)(2,1)S(1)} %all-to-all-done) | copy-start | bytes 1179652
  53.5 17.6 %collective-permute-start.3 = (bf16[128,1536]{1,0:T(8,128)(2,1)S(1)}, bf16[128,1536]{1,0:T(8,128)(2,1)S(1)}, u32[]{:S(2)}, u32[]{:S(2)}) collective-permute-start(bf16[128,1536]{1,0:T(8,128)(2,1)S(1)} %bitcast.28), channel_id=1, source_target_pairs={{0,88},{8,0},{16,8},{24,16},{32,24},{40,32},{48,40},{56,48},{64,56... | collective-permute-start | bytes 1179656 | tf_op jit(solution)/shard_map/ppermute | solution.py:31
  62.8 12.5 %collective-permute-start.4 = (bf16[128,1536]{1,0:T(8,128)(2,1)S(1)}, bf16[128,1536]{1,0:T(8,128)(2,1)S(1)}, u32[]{:S(2)}, u32[]{:S(2)}) collective-permute-start(bf16[128,1536]{1,0:T(8,128)(2,1)S(1)} %bitcast.29), channel_id=1, source_target_pairs={{0,8},{8,16},{16,24},{24,32},{32,40},{40,48},{48,56},{56,64},{64,7... | collective-permute-start | bytes 1179656 | tf_op jit(solution)/shard_map/ppermute | solution.py:31
  66.1 4.5 %collective-permute-start.6 = (s32[256]{0:T(256)S(1)}, s32[256]{0:T(256)S(1)}, u32[]{:S(2)}, u32[]{:S(2)}) collective-permute-start(s32[256]{0:T(256)S(1)} %copy-done.8), channel_id=1, source_target_pairs={{0,4},{4,0},{1,5},{5,1},{2,6},{6,2},{3,7},{7,3},{8,12},{12,8},{9,1... | collective-permute-start | bytes 3080 | tf_op jit(solution)/shard_map/ppermute | solution.py:26
  70.5 5.4 %copy-start.9 = (s32[256]{0:T(256)}, s32[256]{0:T(256)S(1)}, u32[]{:S(2)}) copy-start(s32[256]{0:T(256)S(1)} %collective-permute-done.6) | copy-start | bytes 3076
  71.1 4.8 %copy-start.3 = (bf16[128,1536]{1,0:T(8,128)(2,1)}, bf16[128,1536]{1,0:T(8,128)(2,1)S(1)}, u32[]{:S(2)}) copy-start(bf16[128,1536]{1,0:T(8,128)(2,1)S(1)} %collective-permute-done.3.after) | copy-start | bytes 1179652
  75.3 0.8 copy-start.4
  81.0 7.2 %collective-permute-start.7 = (bf16[16,80,384]{2,1,0:T(8,128)(2,1)}, bf16[16,80,384]{2,1,0:T(8,128)(2,1)S(1)}, u32[]{:S(2)}, u32[]{:S(2)}) collective-permute-start(bf16[16,80,384]{2,1,0:T(8,128)(2,1)} %get-tuple-element.24), channel_id=1, source_target_pairs={{0,4},{4,0},{1,5},{5,1},{2,6},{6,2},{3,7},{7,3},{8,12},{12,8},{9,1... | collective-permute-start | bytes 2949128 | tf_op jit(solution)/shard_map/ppermute | solution.py:26
  90.9 32.2 %all-to-all-start.1 = ((bf16[16,80,384]{2,1,0:T(8,128)(2,1)}), bf16[16,80,384]{2,1,0:T(8,128)(2,1)S(1)}, u32[]{:S(2)}, u32[]{:S(2)}) async-start(bf16[16,80,384]{2,1,0:T(8,128)(2,1)} %add_convert_fusion), calls=%async_computation.1 | async-start | bytes 1966080 | tf_op jit(solution)/shard_map/all_to_all | solution.py:35
  104.1 13.7 %collective-permute-start.9 = (bf16[128,1664]{1,0:T(8,128)(2,1)}, bf16[128,1664]{1,0:T(8,128)(2,1)S(1)}, u32[]{:S(2)}, u32[]{:S(2)}) collective-permute-start(bf16[128,1664]{1,0:T(8,128)(2,1)} %get-tuple-element.28), channel_id=1, source_target_pairs={{0,88},{8,0},{16,8},{24,16},{32,24},{40,32},{48,40},{56,48},{64,56... | collective-permute-start | bytes 1277960 | tf_op jit(solution)/shard_map/ppermute | solution.py:31
  106.1 15.0 %collective-permute-start.8 = (bf16[128,1664]{1,0:T(8,128)(2,1)}, bf16[128,1664]{1,0:T(8,128)(2,1)S(1)}, u32[]{:S(2)}, u32[]{:S(2)}) collective-permute-start(bf16[128,1664]{1,0:T(8,128)(2,1)} %get-tuple-element.27), channel_id=1, source_target_pairs={{0,8},{8,16},{16,24},{24,32},{32,40},{40,48},{48,56},{56,64},{64,7... | collective-permute-start | bytes 1277960 | tf_op jit(solution)/shard_map/ppermute | solution.py:31
  136.8 19.2 %collective-permute-start.11 = (bf16[256,384]{1,0:T(8,128)(2,1)S(1)}, bf16[256,384]{1,0:T(8,128)(2,1)}, u32[]{:S(2)}, u32[]{:S(2)}) collective-permute-start(bf16[256,384]{1,0:T(8,128)(2,1)S(1)} %all_gather.7), channel_id=1, source_target_pairs={{0,192},{192,384},{384,576},{576,0},{1,193},{193,385},{385,577},{5... | collective-permute-start | bytes 589832 | tf_op jit(solution)/shard_map/ppermute | solution.py:31
  141.2 15.8 %collective-permute-start.12 = (bf16[256,384]{1,0:T(8,128)(2,1)S(1)}, bf16[256,384]{1,0:T(8,128)(2,1)}, u32[]{:S(2)}, u32[]{:S(2)}) collective-permute-start(bf16[256,384]{1,0:T(8,128)(2,1)S(1)} %all_gather.7), channel_id=1, source_target_pairs={{0,384},{192,576},{384,0},{576,192},{1,385},{193,577},{385,1},{577... | collective-permute-start | bytes 589832 | tf_op jit(solution)/shard_map/ppermute | solution.py:31
  144.5 36.4 %collective-permute-start.13 = (bf16[256,384]{1,0:T(8,128)(2,1)S(1)}, bf16[256,384]{1,0:T(8,128)(2,1)S(1)}, u32[]{:S(2)}, u32[]{:S(2)}) collective-permute-start(bf16[256,384]{1,0:T(8,128)(2,1)S(1)} %all_gather.7), channel_id=1, source_target_pairs={{0,576},{192,0},{384,192},{576,384},{1,577},{193,1},{385,193},{577... | collective-permute-start | bytes 589832 | tf_op jit(solution)/shard_map/ppermute | solution.py:31
  148.2 23.9 %all-to-all-start.2 = ((bf16[8,16,1664]{2,1,0:T(8,128)(2,1)}), bf16[8,16,1664]{2,1,0:T(8,128)(2,1)S(1)}, u32[]{:S(2)}, u32[]{:S(2)}) async-start(bf16[8,16,1664]{2,1,0:T(8,128)(2,1)} %bitcast.11), calls=%async_computation.2 | async-start | bytes 851968 | tf_op jit(solution)/shard_map/all_to_all | solution.py:35
  153.9 4.1 %collective-permute-start.10 = (f32[24,8,384]{2,1,0:T(8,128)S(1)}, f32[24,8,384]{2,1,0:T(8,128)S(1)}, u32[]{:S(2)}, u32[]{:S(2)}) collective-permute-start(f32[24,8,384]{2,1,0:T(8,128)S(1)} %dynamic-slice_bitcast_fusion), channel_id=1, source_target_pairs={{0,4},{4,0},{1,5},{5,1},{2,6},{6,2},{3,7},{7,3},{8,12},{12,8},{9,1... | collective-permute-start | bytes 884744 | tf_op jit(solution)/shard_map/ppermute | solution.py:26
  158.0 1.1 copy-start.6
  172.1 28.1 %all-to-all-start.3 = ((f32[24,8,384]{2,1,0:T(8,128)}), f32[24,8,384]{2,1,0:T(8,128)S(1)}, u32[]{:S(2)}, u32[]{:S(2)}) async-start(f32[24,8,384]{2,1,0:T(8,128)} %bitcast_add_fusion), calls=%async_computation.3 | async-start | bytes 589824 | tf_op jit(solution)/shard_map/all_to_all | solution.py:35
